TPU v7x, 512 devices: a whole 4x8x8 slice. The times are simulated.
512 devices in a mesh: seq: 64 (over x, y, core), head: 8 (over z).
Axes of the slice: x: 4, y: 8, z: 8, core: 2. Of those that a mesh axis runs over, the one named last changes fastest.
Arguments:
- text_rows: bfloat16 [8192, 4096], P('seq', 'head'), may hold values from -6 to 6
- picture_rows: bfloat16 [2048, 4096], P('seq', 'head'), may hold values from -6 to 6
- picture_slots: int32 [2048], P('seq'), may hold values from 0 to 8191, as said below
- norm_gain: float32 [4096], replicated, may hold values from 0.1 to 1.9
- w_query: bfloat16 [4096, 4096], P('seq', 'head'), may hold values from -1 to 1
- w_key: bfloat16 [4096, 1024], P('seq', 'head'), may hold values from -1 to 1
- w_value: bfloat16 [4096, 1024], P('seq', 'head'), may hold values from -0.09375 to 0.09375
- w_out: bfloat16 [4096, 4096], P('head', 'seq'), may hold values from -0.5 to 0.5
- cache_keys: bfloat16 [4096, 1024], P('seq', 'head'), may hold values from -500 to 500
- cache_values: bfloat16 [4096, 1024], P('seq', 'head'), may hold values from -6 to 6
- recompute_rows: bfloat16 [512, 4096], P('seq', 'head'), may hold values from -6 to 6
- recompute_slots: int32 [512], P('seq'), may hold values from 0 to 4095, as said below
Outputs:
- mixed: bfloat16 [8192, 4096], P('seq', 'head')
Inputs may be any that keep to these rules, and one draw needn't show every extreme that they name: `picture_slots`: distinct stream positions, in runs of 256 consecutive positions, one run a tile; the first tile's run starts at position 4096 and the last tile's run ends at the stream's last position. `recompute_slots`: each aligned block b of 8 entries names distinct rows of cache rows b * 64 to (b + 1) * 64 - 1.
All inputs are finite; a program needn't handle non-finite values.
Results may differ from a plain program's by a relative error of at most 0.02.
Values may be sent and summed in bfloat16 or wider, within the bound.
A program may use at most 128 MiB of HBM per device.

v0:
```python
import jax
import jax.numpy as jnp
from jax import lax
from jax.sharding import PartitionSpec as P

D = 4096
HD = 128


EPSILON = 1e-05
ROPE_BASE = 1000000.0
NEG_FILL = -1e30


def rotate(values, positions):
    half = values.shape[-1] // 2
    freqs = ROPE_BASE ** (-jnp.arange(half, dtype=jnp.float32) / half)
    angles = positions[:, None] * freqs[None, :]
    cosine = jnp.cos(angles)[:, None, :]
    sine = jnp.sin(angles)[:, None, :]
    first = values[..., :half]
    second = values[..., half:]
    return jnp.concatenate(
        [first * cosine - second * sine, second * cosine + first * sine], axis=-1
    )


def scaled(rows_wide, squares, gain):
    return (rows_wide * lax.rsqrt(squares / D + EPSILON)[:, None] * gain[None, :]).astype(
        jnp.bfloat16
    )


def attend(carry, key_piece, value_piece, queries, allowed):
    best, total, accum = carry
    count = key_piece.shape[0]
    kv_local = queries.shape[0]
    keys_split = key_piece.reshape(count, kv_local, HD)
    values_split = value_piece.reshape(count, kv_local, HD)
    scores = jnp.einsum(
        "kgtd,nkd->kgtn", queries, keys_split, preferred_element_type=jnp.float32
    ) * HD ** (-0.5)
    scores = jnp.where(allowed, scores, NEG_FILL)
    fresh = jnp.maximum(best, jnp.max(scores, axis=-1))
    factor = jnp.exp(best - fresh)
    weights = jnp.where(allowed, jnp.exp(scores - fresh[..., None]), 0.0)
    total = total * factor + jnp.sum(weights, axis=-1)
    accum = accum * factor[..., None] + jnp.einsum(
        "kgtn,nkd->kgtd",
        weights.astype(jnp.bfloat16),
        values_split,
        preferred_element_type=jnp.float32,
    )
    return (fresh, total, accum)


def on_device(
    text_rows,
    picture_rows,
    picture_slots,
    norm_gain,
    w_query,
    w_key,
    w_value,
    w_out,
    cache_keys,
    cache_values,
    recompute_rows,
    recompute_slots,
):
    tok_rows = text_rows.shape[0]
    rec_count = recompute_rows.shape[0]
    cache_rows = cache_keys.shape[0]
    seq_index = lax.axis_index("seq")
    local_pos = seq_index * tok_rows + jnp.arange(tok_rows, dtype=jnp.int32)
    rows_piece = lax.all_gather(picture_rows, "seq", axis=0, tiled=True)
    slots_piece = lax.all_gather(picture_slots, "seq", axis=0, tiled=True)
    select = (slots_piece[None, :] == local_pos[:, None]).astype(jnp.bfloat16)
    placed = jnp.dot(select, rows_piece, preferred_element_type=jnp.float32)
    hits = jnp.sum(select.astype(jnp.float32), axis=1)
    added, hits = (placed, hits)
    stream = jnp.where(hits[:, None] > 0.5, added, text_rows.astype(jnp.float32)).astype(
        jnp.bfloat16
    )
    slice_width = stream.shape[1]
    gain_slice = lax.dynamic_slice_in_dim(
        norm_gain, lax.axis_index("head") * slice_width, slice_width, 0
    )
    stream_wide = stream.astype(jnp.float32)
    rec_wide = recompute_rows.astype(jnp.float32)
    stream_sq, rec_sq = lax.psum(
        (jnp.sum(stream_wide * stream_wide, axis=1), jnp.sum(rec_wide * rec_wide, axis=1)), "head"
    )
    normed, rec_normed = (
        lax.all_gather(scaled(stream_wide, stream_sq, gain_slice), "head", axis=1, tiled=True),
        lax.all_gather(scaled(rec_wide, rec_sq, gain_slice), "head", axis=1, tiled=True),
    )
    stacked = jnp.concatenate([normed, rec_normed], axis=0)
    query_cols = w_query.shape[1]
    key_cols = w_key.shape[1]
    pieces = (
        lax.all_gather(w_query, "seq", axis=0, tiled=True),
        lax.all_gather(w_key, "seq", axis=0, tiled=True),
        lax.all_gather(w_value, "seq", axis=0, tiled=True),
    )
    query_all = jnp.dot(stacked, pieces[0], preferred_element_type=jnp.float32)
    key_all = jnp.dot(stacked, pieces[1], preferred_element_type=jnp.float32)
    value_all = jnp.dot(stacked, pieces[2], preferred_element_type=jnp.float32)
    cache_total = cache_rows * lax.axis_size("seq")
    stream_pos = (cache_total + local_pos).astype(jnp.float32)
    rec_pos = recompute_slots.astype(jnp.float32)
    heads_local = query_cols // HD
    kv_local = key_cols // HD
    group = heads_local // kv_local
    rot_query = rotate(query_all[:tok_rows].reshape(tok_rows, heads_local, HD), stream_pos).astype(
        jnp.bfloat16
    )
    rot_key = (
        rotate(key_all[:tok_rows].reshape(tok_rows, kv_local, HD), stream_pos)
        .astype(jnp.bfloat16)
        .reshape(tok_rows, key_cols)
    )
    values_new = value_all[:tok_rows].astype(jnp.bfloat16)
    rot_rec_key = (
        rotate(key_all[tok_rows:].reshape(rec_count, kv_local, HD), rec_pos)
        .astype(jnp.bfloat16)
        .reshape(rec_count, key_cols)
    )
    rec_values = value_all[tok_rows:].astype(jnp.bfloat16)
    local_slots = recompute_slots - seq_index * cache_rows
    select = local_slots[:, None] == jnp.arange(cache_rows, dtype=jnp.int32)[None, :]
    replaced = jnp.any(select, axis=0)[:, None]
    select_cols = select.astype(jnp.bfloat16).T
    new_keys = jnp.dot(select_cols, rot_rec_key, preferred_element_type=jnp.float32).astype(
        jnp.bfloat16
    )
    new_values = jnp.dot(select_cols, rec_values, preferred_element_type=jnp.float32).astype(
        jnp.bfloat16
    )
    cache_k = jnp.where(replaced, new_keys, cache_keys)
    cache_v = jnp.where(replaced, new_values, cache_values)
    queries = jnp.transpose(rot_query.reshape(tok_rows, kv_local, group, HD), (1, 2, 0, 3))
    carry_start = (
        jnp.full((kv_local, group, tok_rows), NEG_FILL, jnp.float32),
        jnp.zeros((kv_local, group, tok_rows), jnp.float32),
        jnp.zeros((kv_local, group, tok_rows, HD), jnp.float32),
    )
    pieces = (
        lax.all_gather(cache_k, "seq", axis=0, tiled=True),
        lax.all_gather(cache_v, "seq", axis=0, tiled=True),
    )
    allowed = jnp.ones((tok_rows, pieces[0].shape[0]), jnp.bool_)
    carry_mid = attend(carry_start, pieces[0], pieces[1], queries, allowed)
    pieces = (
        lax.all_gather(rot_key, "seq", axis=0, tiled=True),
        lax.all_gather(values_new, "seq", axis=0, tiled=True),
    )
    key_pos = jnp.arange(pieces[0].shape[0], dtype=jnp.int32)
    allowed = key_pos[None, :] <= local_pos[:, None]
    best, total, accum = attend(carry_mid, pieces[0], pieces[1], queries, allowed)
    attended = (
        jnp.transpose(accum / total[..., None], (2, 0, 1, 3))
        .reshape(tok_rows, query_cols)
        .astype(jnp.bfloat16)
    )
    partial_out = jnp.dot(
        attended,
        lax.all_gather(w_out, "seq", axis=1, tiled=True),
        preferred_element_type=jnp.float32,
    )
    return lax.psum_scatter(
        partial_out.astype(jnp.bfloat16), "head", scatter_dimension=1, tiled=True
    )


def solution(mesh):
    return jax.shard_map(
        on_device,
        mesh=mesh,
        in_specs=(
            P("seq", "head"),
            P("seq", "head"),
            P("seq"),
            P(),
            P("seq", "head"),
            P("seq", "head"),
            P("seq", "head"),
            P("head", "seq"),
            P("seq", "head"),
            P("seq", "head"),
            P("seq", "head"),
            P("seq"),
        ),
        out_specs=P("seq", "head"),
        check_vma=False,
    )
```

profile of v0, /device:TPU:7, one launch (start us, length us, event | category | flops | bytes accessed | tf_op | source)
XLA Modules:
  0.0 873.1 jit_solution(5738790809692181335)
XLA Ops:
  6.5 0.7 all-gather.11.cloned.1.call-update
  7.3 1.3 dynamic-slice
  9.2 0.8 dynamic_slice.3
  10.0 0.8 dynamic-update-slice
  10.8 15.5 %all-reduce = s32[2048]{0:T(1024)S(1)} all-reduce(s32[2048]{0:T(1024)S(1)} %dynamic-update-slice), channel_id=1, replica_groups=mesh['seq'=64,'head'=8] {'seq'}, use_global_device_ids=true, to_apply=%add | all-reduce | flops 2048 | bytes 16384
  26.4 0.8 fusion.60
  27.2 0.3 convert_reduce_fusion
  27.4 69.9 %all-gather.11.cloned.1.call-done = bf16[2048,512]{1,0:T(8,128)(2,1)} async-done(((bf16[32,512]{1,0:T(8,128)(2,1)}), bf16[2048,512]{1,0:T(8,128)(2,1)}) %all-gather.11.cloned.1.call-update) | async-done | bytes 2097168 | tf_op jit(solution)/shard_map/all_gather | solution.py:76
  97.3 2.2 multiply_reduce_fusion.1
  99.5 14.4 %all-reduce.1 = (f32[128]{0:T(128)S(1)}, f32[8]{0:T(128)S(1)}) all-reduce(f32[128]{0:T(128)S(1)} %get-tuple-element.24, f32[8]{0:T(128)S(1)} %fusion.60), channel_id=1, replica_groups=mesh['seq'=64,'head'=8] {'head'}, use_global_device_ids=true, to_apply=%region_2.3 | all-reduce | flops 136 | bytes 1088 | tf_op jit(solution)/shard_map/psum | solution.py:91
  113.9 0.8 multiply_convert_fusion
  114.7 0.7 all-gather.17.cloned.1.call-update
  115.4 0.5 all-gather.21.cloned.1.call-update
  116.0 0.5 all-gather.15.cloned.1.call-update
  116.6 0.7 fusion.89
  117.4 0.8 fusion.62
  118.2 18.7 %all_gather.39 = bf16[8,4096]{1,0:T(8,128)(2,1)S(1)} all-gather(bf16[8,512]{1,0:T(8,128)(2,1)S(1)} %fusion.62), channel_id=1, replica_groups=mesh['seq'=64,'head'=8] {'head'}, dimensions={1}, use_global_device_ids=true | all-gather | bytes 73728 | tf_op jit(solution)/shard_map/all_gather | solution.py:96
  136.9 14.6 %all-gather.13.cloned.1.call-done = bf16[128,4096]{1,0:T(8,128)(2,1)} async-done(((bf16[128,512]{1,0:T(8,128)(2,1)}), bf16[128,4096]{1,0:T(8,128)(2,1)}) %all-gather.13.cloned.1.call-update) | async-done | bytes 1048592 | tf_op jit(solution)/shard_map/all_gather | solution.py:95
  151.4 1.3 constant_dynamic-update-slice_fusion.1
  152.8 85.8 %all-gather.17.cloned.1.call-done = bf16[4096,128]{1,0:T(8,128)(2,1)} async-done(((bf16[64,128]{1,0:T(8,128)(2,1)}), bf16[4096,128]{1,0:T(8,128)(2,1)}) %all-gather.17.cloned.1.call-update) | async-done | bytes 1048592 | tf_op jit(solution)/shard_map/all_gather | solution.py:103
  238.5 1.7 fusion.90
  240.2 0.1 fusion.79
  240.4 1.6 fusion.33
  242.0 0.3 fusion.59
  242.4 0.7 pad_maximum_fusion
  243.1 78.3 %all-gather.21.cloned.1.call-done = bf16[4096,128]{1,0:T(8,128)(2,1)} async-done(((bf16[64,128]{1,0:T(8,128)(2,1)}), bf16[4096,128]{1,0:T(8,128)(2,1)}) %all-gather.21.cloned.1.call-update) | async-done | bytes 1048592 | tf_op jit(solution)/shard_map/all_gather | solution.py:104
  321.4 1.7 convolution_convert_fusion.1
  323.1 0.6 slice.55
  323.8 0.9 fusion.34
  324.7 0.5 all-gather.29.cloned.1.call-update
  325.3 0.3 multiply_cosine_fusion.1
  325.6 0.7 iota_compare_fusion
  326.3 80.3 %all-gather.15.cloned.1.call-done = bf16[4096,512]{1,0:T(8,128)(2,1)} async-done(((bf16[64,512]{1,0:T(8,128)(2,1)}), bf16[4096,512]{1,0:T(8,128)(2,1)}) %all-gather.15.cloned.1.call-update) | async-done | bytes 4194320 | tf_op jit(solution)/shard_map/all_gather | solution.py:102
  406.6 2.9 fusion.41
  409.6 0.2 fusion.88
  409.8 79.6 %all-gather.19.cloned.1.call-done = bf16[4096,128]{1,0:T(8,128)(2,1)} async-done(((bf16[64,128]{1,0:T(8,128)(2,1)}), bf16[4096,128]{1,0:T(8,128)(2,1)}) %all-gather.19.cloned.1.call-update) | async-done | bytes 1048592 | tf_op jit(solution)/shard_map/all_gather | solution.py:149
  489.4 5.7 multiply_reduce_fusion
  495.2 78.3 %all-gather.25.cloned.1.call-done = bf16[8192,128]{1,0:T(8,128)(2,1)} async-done(((bf16[128,128]{1,0:T(8,128)(2,1)}), bf16[8192,128]{1,0:T(8,128)(2,1)}) %all-gather.25.cloned.1.call-update) | async-done | bytes 2097168 | tf_op jit(solution)/shard_map/all_gather | solution.py:155
  573.5 5.0 fusion
  578.5 1.5 fusion.6
  580.0 5.0 fusion.1
  585.0 72.4 %all-gather.27.cloned.1.call-done = bf16[8192,128]{1,0:T(8,128)(2,1)} async-done(((bf16[128,128]{1,0:T(8,128)(2,1)}), bf16[8192,128]{1,0:T(8,128)(2,1)}) %all-gather.27.cloned.1.call-update) | async-done | bytes 2097168 | tf_op jit(solution)/shard_map/all_gather | solution.py:156
  657.4 9.9 %fusion.3 = f32[4,128,128]{1,2,0:T(8,128)S(1)} fusion(f32[4,128,8192]{2,1,0:T(8,128)} %copy-done, f32[4,128]{1,0:T(4,128)S(1)} %get-tuple-element.18, pred[128,8192]{1,0:T(8,128)(4,1)S(1)} %iota_compare_fusion, bf16[8192,128]{1,0:T(8,128)(2,1)} %all-gather.27.cloned.1.call-done), kind=kOutput, calls=%fused_computation.6 | convolution fusion | flops 1094713344 | bytes 20187136 | tf_op jit(solution)/shard_map/kgtn,nkd->kgtd/dot_general | solution.py:48
  667.3 73.0 %all-gather.23.cloned.1.call-done = bf16[4096,128]{1,0:T(8,128)(2,1)} async-done(((bf16[64,128]{1,0:T(8,128)(2,1)}), bf16[4096,128]{1,0:T(8,128)(2,1)}) %all-gather.23.cloned.1.call-update) | async-done | bytes 1048592 | tf_op jit(solution)/shard_map/all_gather | solution.py:150
  740.3 5.4 fusion.38
  745.7 79.7 %all-gather.29.cloned.1.call-done = bf16[512,4096]{0,1:T(8,128)(2,1)} async-done(((bf16[512,64]{0,1:T(8,128)(2,1)}), bf16[512,4096]{0,1:T(8,128)(2,1)}) %all-gather.29.cloned.1.call-update) | async-done | bytes 4194320 | tf_op jit(solution)/shard_map/all_gather | solution.py:168
  825.4 4.7 convolution_convert_fusion
  830.1 36.4 %reduce-scatter.2.cloned.1.call-done = bf16[128,512]{1,0:T(8,128)(2,1)} async-done(((bf16[128,4096]{1,0:T(8,128)(2,1)}), bf16[128,512]{1,0:T(8,128)(2,1)}) %reduce-scatter.2.cloned.1.call-update) | async-done | bytes 131088 | tf_op jit(solution)/shard_map/reduce_scatter | solution.py:171
  (38 shorter events, 0.8 us)
Async XLA Ops:
  6.5 317.2 %copy-start.2 = (bf16[64,128]{1,0:T(8,128)(2,1)S(1)}, bf16[64,128]{1,0:T(8,128)(2,1)}, u32[]{:S(2)}) copy-start(bf16[64,128]{1,0:T(8,128)(2,1)} %param.21) | copy-start | bytes 49156
  6.5 90.8 %all-gather.11.cloned.1.call-start = ((), (), s32[]{:S(2)}) async-start(), calls=%async_computation.1 | async-start | bytes 2129920 | tf_op jit(solution)/shard_map/all_gather | solution.py:76
  7.3 144.2 %all-gather.13.cloned.1.call-start = ((), (), s32[]{:S(2)}) async-start(), calls=%async_computation.2 | async-start | bytes 1179648 | tf_op jit(solution)/shard_map/all_gather | solution.py:95
  114.7 123.9 %all-gather.17.cloned.1.call-start = ((), (), s32[]{:S(2)}) async-start(), calls=%async_computation.4 | async-start | bytes 1064960 | tf_op jit(solution)/shard_map/all_gather | solution.py:103
  115.4 206.0 %all-gather.21.cloned.1.call-start = ((), (), s32[]{:S(2)}) async-start(), calls=%async_computation.6 | async-start | bytes 1064960 | tf_op jit(solution)/shard_map/all_gather | solution.py:104
  116.0 290.6 %all-gather.15.cloned.1.call-start = ((), (), s32[]{:S(2)}) async-start(), calls=%async_computation.3 | async-start | bytes 4259840 | tf_op jit(solution)/shard_map/all_gather | solution.py:102
  116.6 372.9 %all-gather.19.cloned.1.call-start = ((), (), s32[]{:S(2)}) async-start(), calls=%async_computation.5 | async-start | bytes 1064960 | tf_op jit(solution)/shard_map/all_gather | solution.py:149
  242.0 331.5 %all-gather.25.cloned.1.call-start = ((), (), s32[]{:S(2)}) async-start(), calls=%async_computation.8 | async-start | bytes 2129920 | tf_op jit(solution)/shard_map/all_gather | solution.py:155
  243.1 414.3 %all-gather.27.cloned.1.call-start = ((), (), s32[]{:S(2)}) async-start(), calls=%async_computation.9 | async-start | bytes 2129920 | tf_op jit(solution)/shard_map/all_gather | solution.py:156
  323.7 416.6 %all-gather.23.cloned.1.call-start = ((), (), s32[]{:S(2)}) async-start(), calls=%async_computation.7 | async-start | bytes 1064960 | tf_op jit(solution)/shard_map/all_gather | solution.py:150
  324.7 500.8 %all-gather.29.cloned.1.call-start = ((), (), s32[]{:S(2)}) async-start(), calls=%async_computation.10 | async-start | bytes 4259840 | tf_op jit(solution)/shard_map/all_gather | solution.py:168
  325.3 541.3 %reduce-scatter.2.cloned.1.call-start = ((), (), s32[]{:S(2)}) async-start(), calls=%async_computation.11 | async-start | bytes 1179648 | tf_op jit(solution)/shard_map/reduce_scatter | solution.py:171
  573.5 5.0 copy-start.1
  578.5 6.5 copy-start
Sparse Core Ops, SparseCore 0:
  10.7 86.5 all-gather.10
  114.8 36.6 all-gather.12
  154.8 83.6 all-gather.16
  241.8 79.6 all-gather.20
  324.6 81.8 all-gather.14
  409.8 79.6 all-gather.18
  492.8 80.6 all-gather.24
  576.8 80.5 all-gather.26
  660.8 79.4 all-gather.22
  743.5 81.8 all-gather.28
  830.3 36.2 reduce-scatter.1
where the time goes:
time: 878 us; the launch traced here: 873 us
  waiting for transfers between devices  751 us (86%)
  blocking collectives  48.6 us (6%)
  matrix products  41.5 us (5%)
  between operations  14.1 us (2%)
  other arithmetic  12.1 us (1%)
    all_gather x1, waiting for transfers between devices, on_device(): lax.all_gather(w_key, 'seq', axis=0, tiled=True)  85.8 us
    all_gather x1, waiting for transfers between devices, on_device(): lax.all_gather(w_query, 'seq', axis=0, tiled=True)  80.3 us
    all_gather x1, waiting for transfers between devices, on_device(): lax.all_gather(w_out, 'seq', axis=1, tiled=True)  79.7 us
    all_gather x1, waiting for transfers between devices, on_device(): lax.all_gather(cache_k, 'seq', axis=0, tiled=True)  79.6 us
    all_gather x1, waiting for transfers between devices, on_device(): lax.all_gather(rot_key, 'seq', axis=0, tiled=True)  78.3 us
    all_gather x1, waiting for transfers between devices, on_device(): lax.all_gather(w_value, 'seq', axis=0, tiled=True)  78.3 us
    all_gather x1, waiting for transfers between devices, on_device(): lax.all_gather(cache_v, 'seq', axis=0, tiled=True)  73 us
    all_gather x1, waiting for transfers between devices, on_device(): lax.all_gather(values_new, 'seq', axis=0, tiled=True)  72.4 us
  transfers between devices with their start and end apart: 11, of which 11 were waited for; matrix products, arithmetic and copies ran while one was open for 6% of the time, Pallas kernels for 0%

commit v1 on v0

v1 whole, which is shorter than its diff:
```python
import functools
import math

import jax
import jax.numpy as jnp
from jax import lax
from jax.experimental import pallas as pl
from jax.experimental.pallas import tpu as pltpu
from jax.sharding import PartitionSpec as P

D = 4096
HD = 128
NX, NY, NC, NZ = 4, 8, 2, 8
MESH = pl.DeviceIdType.MESH

EPSILON = 1e-05
ROPE_BASE = 1000000.0
NEG_FILL = -1e30


def rotate(values, positions):
    half = values.shape[-1] // 2
    freqs = ROPE_BASE ** (-jnp.arange(half, dtype=jnp.float32) / half)
    angles = positions[:, None] * freqs[None, :]
    cosine = jnp.cos(angles)[:, None, :]
    sine = jnp.sin(angles)[:, None, :]
    first = values[..., :half]
    second = values[..., half:]
    return jnp.concatenate(
        [first * cosine - second * sine, second * cosine + first * sine], axis=-1
    )


def place():
    s = lax.axis_index("seq")
    return s // (NY * NC), (s // NC) % NY, s % NC


def seq_of(x, y, c):
    return ((x % NX) * NY + y % NY) * NC + c


class Sends:
    def __init__(self, send_sems, recv_sems):
        self.send_sems, self.recv_sems, self.made = send_sems, recv_sems, []

    def start(self, src, dst, device_id):
        at = len(self.made)
        copy = pltpu.make_async_remote_copy(
            src_ref=src,
            dst_ref=dst,
            send_sem=self.send_sems.at[at],
            recv_sem=self.recv_sems.at[at],
            device_id=device_id,
            device_id_type=MESH,
        )
        copy.start()
        self.made.append(copy)
        return copy

    def finish(self):
        for copy in self.made:
            copy.wait_send()


def wait_all(copies):
    for copy in copies:
        copy.wait_recv()


PLANE_COPIES = 58
LINE_COPIES = 7


def plane_steps(src, out, sends, local_sem):
    x, y, c = place()
    half = src.shape[0] // 2
    a_rows, b_rows = pl.ds(0, half), pl.ds(half, half)
    every_x = pl.ds(0, NX)
    up = {"seq": seq_of(x, y + 1, c)}
    down = {"seq": seq_of(x, y + NY - 1, c)}
    right = {"seq": seq_of(x + 1, y, c)}
    left = {"seq": seq_of(x + NX - 1, y, c)}
    other = {"seq": seq_of(x, y, 1 - c)}

    def col(k):
        return (y + k + NY) % NY

    def a_block(xs, k):
        return out.at[xs, col(k), c, a_rows]

    def b_block(xx, k):
        return out.at[xx, col(k), c, b_rows]

    def spread(k):
        block = b_block(x, k)
        return [sends.start(block, block, right), sends.start(block, block, left)]

    def forward(k):
        odd = col(k) % 2
        block = b_block((x + NX - 1 + 2 * odd) % NX, k)
        return sends.start(block, block, {"seq": seq_of(x + 1 + 2 * odd, y, c)})

    def hand(ref):
        return sends.start(ref, ref, other)

    own = pltpu.make_async_copy(src, out.at[x, y, c], local_sem)
    own.start()
    along = [
        sends.start(src.at[a_rows], a_block(x, 0), {"seq": seq_of(x + d, y, c)}) for d in (1, 2, 3)
    ]
    own.wait()
    ring_b = [sends.start(b_block(x, 0), b_block(x, 0), to) for to in (up, down)]
    spreads = {0: spread(0)}
    forwards, handed = {}, []
    ring_a = []
    yield
    for k in range(1, NY // 2 + 3):
        if k == 1:
            wait_all(along)
        elif k <= NY // 2 + 1:
            wait_all(ring_a)
        if k <= NY // 2:
            if k < NY // 2:
                parts = (every_x, every_x)
            else:
                parts = (pl.ds(0, NX // 2), pl.ds(NX // 2, NX // 2))
            ring_a = [
                sends.start(a_block(parts[0], 1 - k), a_block(parts[0], 1 - k), up),
                sends.start(a_block(parts[1], k - 1), a_block(parts[1], k - 1), down),
            ]
        if k == 1:
            handed.append(hand(a_block(every_x, 0)))
        elif k <= NY // 2:
            handed.append(hand(a_block(every_x, 1 - k)))
            handed.append(hand(a_block(every_x, k - 1)))
        elif k == NY // 2 + 1:
            handed.append(hand(a_block(every_x, k - 1)))
        if k <= NY // 2:
            wait_all(ring_b)
            if k < NY // 2:
                ring_b = [sends.start(b_block(x, -k), b_block(x, -k), up)]
                if k < NY // 2 - 1:
                    ring_b.append(sends.start(b_block(x, k), b_block(x, k), down))
                for j in (-k, k):
                    spreads[j] = spread(j)
            else:
                spreads[-k] = spread(-k)
        arrived = k - 1
        if arrived <= NY // 2:
            for j in {0: (0,), NY // 2: (-NY // 2,)}.get(arrived, (-arrived, arrived)):
                wait_all(spreads[j])
                forwards[j] = forward(j)
        arrived = k - 2
        if arrived >= 0:
            for j in {0: (0,), NY // 2: (-NY // 2,)}.get(arrived, (-arrived, arrived)):
                wait_all([forwards[j]])
                handed.append(hand(b_block(every_x, j)))
        yield
    wait_all(handed)


def line_steps(src, out, sends, local_sem):
    z = lax.axis_index("head")
    up = {"head": (z + 1) % NZ}
    down = {"head": (z + NZ - 1) % NZ}

    def block(k):
        return out.at[(z + k + NZ) % NZ]

    own = pltpu.make_async_copy(src, block(0), local_sem)
    own.start()
    ring = [sends.start(src, block(0), to) for to in (up, down)]
    own.wait()
    yield
    for k in range(1, NZ // 2 + 1):
        wait_all(ring)
        ring = []
        if k < NZ // 2:
            ring.append(sends.start(block(-k), block(-k), up))
        if k < NZ // 2 - 1:
            ring.append(sends.start(block(k), block(k), down))
        yield


def greet(plane, line):
    x, y, c = place()
    z = lax.axis_index("head")
    partners = []
    if plane:
        partners += [{"seq": seq_of(x + d, y, c)} for d in (1, 2, 3)]
        partners += [{"seq": seq_of(x, y + d, c)} for d in (1, NY - 1)]
        partners += [{"seq": seq_of(x, y, 1 - c)}]
    partners += [{"head": (z + d) % NZ} for d in line]
    barrier = pltpu.get_barrier_semaphore()
    for partner in partners:
        pl.semaphore_signal(barrier, inc=1, device_id=partner, device_id_type=MESH)
    pl.semaphore_wait(barrier, len(partners))


def gather_kernel(planes, lines, *refs):
    total = planes + lines
    ins, outs = refs[:total], refs[total : 2 * total]
    send_sems, recv_sems, local_sems = refs[2 * total :]
    greet(planes > 0, (1, NZ - 1) if lines else ())
    sends = Sends(send_sems, recv_sems)
    runs = [plane_steps(ins[i], outs[i], sends, local_sems.at[i]) for i in range(planes)]
    runs += [line_steps(ins[i], outs[i], sends, local_sems.at[i]) for i in range(planes, total)]
    while runs:
        runs = [run for run in runs if next(run, runs) is not runs]
    sends.finish()


def gather(plane_arrays, line_arrays, collective_id):
    arrays = list(plane_arrays) + list(line_arrays)
    copies = PLANE_COPIES * len(plane_arrays) + LINE_COPIES * len(line_arrays)
    shapes = [(NX, NY, NC) + a.shape for a in plane_arrays] + [(NZ,) + a.shape for a in line_arrays]
    anywhere = pl.BlockSpec(memory_space=pl.ANY)
    return pl.pallas_call(
        functools.partial(gather_kernel, len(plane_arrays), len(line_arrays)),
        out_shape=[jax.ShapeDtypeStruct(shape, jnp.bfloat16) for shape in shapes],
        in_specs=[anywhere] * len(arrays),
        out_specs=[anywhere] * len(arrays),
        scratch_shapes=[
            pltpu.SemaphoreType.DMA((copies,)),
            pltpu.SemaphoreType.DMA((copies,)),
            pltpu.SemaphoreType.DMA((len(arrays),)),
        ],
        compiler_params=pltpu.CompilerParams(collective_id=collective_id, has_side_effects=True),
    )(*arrays)


def exchange_kernel(src, out, send_sems, recv_sems, local_sem):
    z = lax.axis_index("head")
    greet(False, range(1, NZ))
    own = pltpu.make_async_copy(src.at[z], out.at[0], local_sem)
    own.start()
    copies = []
    for d in range(1, NZ):
        copy = pltpu.make_async_remote_copy(
            src_ref=src.at[(z + d) % NZ],
            dst_ref=out.at[d],
            send_sem=send_sems.at[d],
            recv_sem=recv_sems.at[d],
            device_id={"head": (z + d) % NZ},
            device_id_type=MESH,
        )
        copy.start()
        copies.append(copy)
    own.wait()
    for copy in copies:
        copy.wait()


def exchange(blocks, collective_id):
    anywhere = pl.BlockSpec(memory_space=pl.ANY)
    return pl.pallas_call(
        exchange_kernel,
        out_shape=jax.ShapeDtypeStruct(blocks.shape, blocks.dtype),
        in_specs=[anywhere],
        out_specs=anywhere,
        scratch_shapes=[
            pltpu.SemaphoreType.DMA((NZ,)),
            pltpu.SemaphoreType.DMA((NZ,)),
            pltpu.SemaphoreType.DMA,
        ],
        compiler_params=pltpu.CompilerParams(collective_id=collective_id, has_side_effects=True),
    )(blocks)


def attend_kernel(tok, cache, group, q_ref, kv_ref, o_ref, best, total, accum):
    step = pl.program_id(0)
    s = lax.axis_index("seq")
    span = kv_ref.shape[0]
    rows = cache + tok
    scale = HD**-0.5 * math.log2(math.e)

    @pl.when(step == 0)
    def _():
        best[...] = jnp.full_like(best, NEG_FILL)
        total[...] = jnp.zeros_like(total)
        accum[...] = jnp.zeros_like(accum)

    def update(keys, values, mask):
        scores = lax.dot_general(
            q_ref[...], keys, (((1,), (1,)), ((), ())), preferred_element_type=jnp.float32
        )
        if mask is not None:
            scores = jnp.where(mask, scores, NEG_FILL)
        old = best[...]
        fresh = jnp.maximum(old, jnp.max(scores, axis=1, keepdims=True))
        factor = jnp.exp2((old - fresh) * scale)
        weights = jnp.exp2((scores - fresh) * scale)
        best[...] = fresh
        total[...] = total[...] * factor + jnp.sum(weights, axis=1, keepdims=True)
        accum[...] = accum[...] * factor + jnp.dot(
            weights.astype(jnp.bfloat16), values, preferred_element_type=jnp.float32
        )

    def whole():
        block = kv_ref[...]
        return (
            block[:, :, :HD].reshape(span * rows, HD),
            block[:, :, HD:].reshape(span * rows, HD),
        )

    @pl.when(step < s // span)
    def _():
        keys, values = whole()
        update(keys, values, None)

    @pl.when(step == s // span)
    def _():
        keys, values = whole()
        at = lax.broadcasted_iota(jnp.int32, (1, span * rows), 1)
        row = at % rows
        key_pos = jnp.where(row < cache, -1, (step * span + at // rows) * tok + row - cache)
        query_at = lax.broadcasted_iota(jnp.int32, (group * tok, 1), 0)
        query_pos = s * tok + query_at % tok
        update(keys, values, key_pos <= query_pos)

    @pl.when(step > s // span)
    def _():
        block = kv_ref[:, :cache, :]
        update(
            block[:, :, :HD].reshape(span * cache, HD),
            block[:, :, HD:].reshape(span * cache, HD),
            None,
        )

    @pl.when(step == pl.num_programs(0) - 1)
    def _():
        out = accum[...] / total[...]
        for g in range(group):
            o_ref[:, g * HD : (g + 1) * HD] = out[g * tok : (g + 1) * tok].astype(o_ref.dtype)


def attend(queries, kv, tok, cache, group):
    span = 8
    blocks, rows, width = kv.shape
    return pl.pallas_call(
        functools.partial(attend_kernel, tok, cache, group),
        out_shape=jax.ShapeDtypeStruct((tok, group * HD), jnp.bfloat16),
        grid=(blocks // span,),
        in_specs=[
            pl.BlockSpec((group * tok, HD), lambda i: (0, 0)),
            pl.BlockSpec((span, rows, width), lambda i: (i, 0, 0)),
        ],
        out_specs=pl.BlockSpec((tok, group * HD), lambda i: (0, 0)),
        scratch_shapes=[
            pltpu.VMEM((group * tok, 1), jnp.float32),
            pltpu.VMEM((group * tok, 1), jnp.float32),
            pltpu.VMEM((group * tok, HD), jnp.float32),
        ],
        compiler_params=pltpu.CompilerParams(vmem_limit_bytes=40 * 1024 * 1024),
    )(queries, kv)


def on_device(
    text_rows,
    picture_rows,
    picture_slots,
    norm_gain,
    w_query,
    w_key,
    w_value,
    w_out,
    cache_keys,
    cache_values,
    recompute_rows,
    recompute_slots,
):
    tok_rows, slice_width = text_rows.shape
    rec_count = recompute_rows.shape[0]
    cache_rows = cache_keys.shape[0]
    query_cols = w_query.shape[1]
    key_cols = w_key.shape[1]
    group = query_cols // HD
    seq_index = lax.axis_index("seq")
    local_pos = seq_index * tok_rows + jnp.arange(tok_rows, dtype=jnp.int32)
    digits = jnp.stack([picture_slots // HD, picture_slots % HD], axis=1).astype(jnp.bfloat16)
    digits = jnp.pad(digits, ((0, 0), (0, HD - 2)))
    (pictures,) = gather([jnp.concatenate([picture_rows, digits], axis=1)], [], 0)
    pictures = pictures.reshape(-1, slice_width + HD)
    digits = pictures[:, slice_width : slice_width + 2].astype(jnp.int32)
    slots = digits[:, 0] * HD + digits[:, 1]
    select = (slots[None, :] == local_pos[:, None]).astype(jnp.bfloat16)
    placed = jnp.dot(select, pictures[:, :slice_width], preferred_element_type=jnp.float32)
    hits = jnp.sum(select.astype(jnp.float32), axis=1)
    stream = jnp.where(hits[:, None] > 0.5, placed, text_rows.astype(jnp.float32)).astype(
        jnp.bfloat16
    )
    raw = jnp.concatenate([stream, recompute_rows], axis=0)
    weights = jnp.concatenate([w_query, w_key, w_value, w_out.T], axis=1)
    weights, raw = gather([weights], [raw], 1)
    weights = weights.reshape(D, -1)
    raw = jnp.transpose(raw, (1, 0, 2)).reshape(tok_rows + rec_count, D)
    wide = raw.astype(jnp.float32)
    squares = jnp.sum(wide * wide, axis=1)
    normed = (wide * lax.rsqrt(squares / D + EPSILON)[:, None] * norm_gain[None, :]).astype(
        jnp.bfloat16
    )
    in_cols = query_cols + 2 * key_cols
    projected = jnp.dot(normed, weights[:, :in_cols], preferred_element_type=jnp.float32)
    heads = projected[:, : query_cols + key_cols].reshape(-1, group + 1, HD)
    cache_total = cache_rows * lax.axis_size("seq")
    positions = jnp.concatenate([cache_total + local_pos, recompute_slots]).astype(jnp.float32)
    rotated = rotate(heads, positions).astype(jnp.bfloat16)
    values = projected[:, query_cols + key_cols :].astype(jnp.bfloat16)
    kv = jnp.concatenate([rotated[:, group], values], axis=1)
    local_slots = recompute_slots - seq_index * cache_rows
    select = local_slots[:, None] == jnp.arange(cache_rows, dtype=jnp.int32)[None, :]
    replaced = jnp.any(select, axis=0)[:, None]
    fresh = jnp.dot(
        select.astype(jnp.bfloat16).T, kv[tok_rows:], preferred_element_type=jnp.float32
    ).astype(jnp.bfloat16)
    cache = jnp.where(replaced, fresh, jnp.concatenate([cache_keys, cache_values], axis=1))
    (kv_all,) = gather([jnp.concatenate([cache, kv[:tok_rows]], axis=0)], [], 2)
    queries = jnp.transpose(rotated[:tok_rows, :group], (1, 0, 2)).reshape(group * tok_rows, HD)
    attended = attend(
        queries,
        kv_all.reshape(-1, cache_rows + tok_rows, 2 * HD),
        tok_rows,
        cache_rows,
        group,
    )
    partial_out = lax.dot_general(
        weights[:, in_cols:].reshape(NZ, slice_width, query_cols),
        attended,
        (((2,), (1,)), ((), ())),
        preferred_element_type=jnp.float32,
    ).astype(jnp.bfloat16)
    parts = exchange(jnp.transpose(partial_out, (0, 2, 1)), 3)
    return jnp.sum(parts.astype(jnp.float32), axis=0).astype(jnp.bfloat16)


def solution(mesh):
    return jax.shard_map(
        on_device,
        mesh=mesh,
        in_specs=(
            P("seq", "head"),
            P("seq", "head"),
            P("seq"),
            P(),
            P("seq", "head"),
            P("seq", "head"),
            P("seq", "head"),
            P("head", "seq"),
            P("seq", "head"),
            P("seq", "head"),
            P("seq", "head"),
            P("seq"),
        ),
        out_specs=P("seq", "head"),
        check_vma=False,
    )
```

time: 878 us -> 210 us (0.24)
  waiting for transfers between devices: 751 us -> 0 us
  Pallas kernels: 0 us -> 178 us
  blocking collectives: 48.6 us -> 0 us
  matrix products: 41.5 us -> 8.68 us
  between operations: 14.1 us -> 0.22 us
    all_gather x10 -> x0, waiting for transfers between devices: 712 us -> none  [the longest x1 85.8 us: on_device(): lax.all_gather(w_key, 'seq', axis=0, tiled=True)]
    pallas_call x0 -> x5, Pallas kernels: none -> 178 us  [the longest x3 136 us: gather(): pl.pallas_call(functools.partial(gather_kernel, len(plane_arrays), len(li...]
    reduce_scatter x1 -> x0, waiting for transfers between devices: 36.4 us -> none  [on_device(): lax.psum_scatter(partial_out.astype(jnp.bfloat16), 'head', scatter_dimens...]
    dot_general x11 -> x4, matrix products: 41.5 us -> 8.68 us  [the longest x1 3.89 us: on_device(): jnp.dot(normed, weights[:, :in_cols], preferred_element_type=jnp.float32)]
    all_gather x1 -> x0, blocking collectives: 18.7 us -> none  [on_device(): lax.all_gather(scaled(rec_wide, rec_sq, gain_slice), 'head', axis=1, tile...]
    unnamed x1 -> x0, blocking collectives: 15.5 us -> none
    psum x1 -> x0, blocking collectives: 14.4 us -> none  [on_device(): lax.psum((jnp.sum(stream_wide * stream_wide, axis=1), jnp.sum(rec_wide *...]
  transfers between devices with their start and end apart: 11 -> 0, of which waited for: 11 -> 0; matrix products, arithmetic and copies ran while one was open for 6% -> 0% of each run, Pallas kernels for 0% -> 0%
where the time goes in v1:
time: 210 us; the launch traced here: 209 us
  Pallas kernels  178 us (85%)
  other arithmetic  12.5 us (6%)
  local copies, waits for them, and re-layouts  9.88 us (5%)
  matrix products  8.68 us (4%)
    pallas_call x3, Pallas kernels, gather(): pl.pallas_call(functools.partial(gather_kernel, len(plane_arrays), len(li...  136 us
    pallas_call x1, Pallas kernels, exchange(): pl.pallas_call(exchange_kernel, out_shape=jax.ShapeDtypeStruct(blocks.sha...  28.1 us
    pallas_call x1, Pallas kernels, attend(): pl.pallas_call(functools.partial(attend_kernel, tok, cache, group), out_s...  13.4 us
    slice x1, local copies, waits for them, and re-layouts, on_device(): weights[:, in_cols:].reshape(NZ, slice_width, query_cols)  4.53 us

profile of v1, /device:TPU:7, one launch (start us, length us, event | category | flops | bytes accessed | tf_op | source)
XLA Modules:
  0.0 209.2 jit_solution(1910298572857080638)
XLA Ops:
  0.0 0.7 broadcast_subtract_fusion
  0.7 0.1 fusion.31
  0.8 0.7 add_convert_fusion.1
  1.4 0.7 convert_bitcast_fusion.1
  2.1 0.1 copy.29
  2.2 1.4 fusion.26.refs_0_
  3.6 0.3 multiply_cosine_fusion
  3.9 1.6 pad_maximum_fusion.refs_0_
  5.5 0.0 copy-start.5
  5.5 34.1 %shard_map.118 = bf16[4,8,2,32,640]{4,3,2,1,0:T(8,128)(2,1)} custom-call(bf16[32,640]{1,0:T(8,128)(2,1)} %fusion.26.refs_0_), custom_call_target="tpu_custom_call" | custom-call | tf_op jit(solution)/shard_map/pallas_call | solution.py:219
  39.7 1.1 slice.57
  40.7 0.0 copy-start.4
  40.8 0.2 copy.36
  41.0 0.3 convert_reduce_fusion
  41.3 0.0 copy-done.5
  41.3 2.1 fusion.12
  43.4 0.0 copy-done.4
  43.4 0.7 pad_maximum_fusion.1.refs_1_
  44.0 61.4 %shard_map.119 = (bf16[4,8,2,64,1280]{4,3,2,1,0:T(8,128)(2,1)}, bf16[8,136,512]{2,1,0:T(8,128)(2,1)}) custom-call(bf16[64,1280]{1,0:T(8,128)(2,1)} %pad_maximum_fusion.refs_0_, bf16[136,512]{1,0:T(8,128)(2,1)} %pad_maximum_fusion.1.refs_1_), custom_call_target="tpu_custom_call" | custom-call | tf_op jit(solution)/shard_map/pallas_call | solution.py:219
  105.4 1.6 fusion.2
  107.0 1.5 convert_bitcast_fusion
  108.6 0.0 copy-start.6
  108.6 0.2 copy.39
  108.8 0.5 copy-done.6
  109.3 3.9 %fusion = f32[136,768]{1,0:T(8,128)S(1)} fusion(bf16[4096,1280]{1,0:T(8,128)(2,1)} %bitcast.31, f32[136,4096]{1,0:T(8,128)S(1)} %bitcast.30, f32[4096]{0:T(1024)S(1)} %copy-done.6, f32[136]{0:T(256)S(1)} %add_rsqrt_fusion), kind=kOutput, calls=%fused_computation | convolution fusion | flops 857309184 | bytes 8954400 | tf_op jit(solution)/shard_map/dot_general | solution.py:404
  113.2 4.5 %slice.61 = bf16[4096,512]{1,0:T(8,128)(2,1)} slice(bf16[4096,1280]{1,0:T(8,128)(2,1)} %bitcast.32), slice={[0:4096], [768:1280]} | slice | bytes 8388608 | tf_op jit(solution)/shard_map/slice | solution.py:428
  117.8 0.1 reshape.120
  117.8 0.0 copy-start.2
  117.8 0.0 copy-start.3
  117.8 0.2 fusion.36
  118.0 0.1 add_convert_fusion
  118.2 0.1 fusion.27
  118.3 0.1 fusion.22
  118.4 0.1 copy-done.2
  118.5 0.0 copy-done.3
  118.6 0.3 fusion.19
  118.8 0.7 fusion.24.refs_0_
  119.5 40.9 %shard_map.120 = bf16[4,8,2,192,256]{4,3,2,1,0:T(8,128)(2,1)} custom-call(bf16[192,256]{1,0:T(8,128)(2,1)} %fusion.24.refs_0_), custom_call_target="tpu_custom_call" | custom-call | tf_op jit(solution)/shard_map/pallas_call | solution.py:219
  160.4 0.0 copy-start
  160.4 2.8 %copy-done = bf16[4,8,2,192,256]{4,3,2,1,0:T(8,128)(2,1)S(1)} copy-done((bf16[4,8,2,192,256]{4,3,2,1,0:T(8,128)(2,1)S(1)}, bf16[4,8,2,192,256]{4,3,2,1,0:T(8,128)(2,1)}, u32[]{:S(2)}) %copy-start) | copy-done | bytes 6291480
  163.2 0.0 copy-start.1
  163.2 13.4 %shard_map.121 = bf16[128,512]{1,0:T(8,128)(2,1)S(1)} custom-call(bf16[512,128]{1,0:T(8,128)(2,1)S(1)} %bitcast.26, bf16[64,192,256]{2,1,0:T(8,128)(2,1)S(1)} %bitcast.25), custom_call_target="tpu_custom_call" | custom-call | tf_op jit(solution)/shard_map/pallas_call | solution.py:341
  176.6 0.0 copy-done.1
  176.6 2.4 %fusion.5.src = bf16[8,128,512]{2,1,0:T(8,128)(2,1)} fusion(bf16[8,512,512]{2,1,0:T(8,128)(2,1)S(1)} %bitcast.27, bf16[128,512]{1,0:T(8,128)(2,1)S(1)} %shard_map.121), kind=kOutput, calls=%fused_computation.9 | convolution fusion | flops 537395200 | bytes 5373952 | tf_op jit(solution)/shard_map/dot_general | solution.py:427
  179.1 28.1 %shard_map.122 = bf16[8,128,512]{2,1,0:T(8,128)(2,1)} custom-call(bf16[8,128,512]{2,1,0:T(8,128)(2,1)} %fusion.5.src), custom_call_target="tpu_custom_call" | custom-call | tf_op jit(solution)/shard_map/pallas_call | solution.py:257
  207.2 2.1 reduce_sum.32
  (9 shorter events, 0.1 us)
Async XLA Ops:
  5.5 35.8 %copy-start.5 = (bf16[128,512]{1,0:T(8,128)(2,1)S(1)}, bf16[128,512]{1,0:T(8,128)(2,1)}, u32[]{:S(2)}) copy-start(bf16[128,512]{1,0:T(8,128)(2,1)} %param.12) | copy-start | bytes 393220
  40.7 2.6 %copy-start.4 = (bf16[8,512]{1,0:T(8,128)(2,1)S(1)}, bf16[8,512]{1,0:T(8,128)(2,1)}, u32[]{:S(2)}) copy-start(bf16[8,512]{1,0:T(8,128)(2,1)} %param.22) | copy-start | bytes 24580
  108.6 0.7 copy-start.6
  117.8 0.7 copy-start.2
  117.8 0.7 copy-start.3
  160.4 2.8 %copy-start = (bf16[4,8,2,192,256]{4,3,2,1,0:T(8,128)(2,1)S(1)}, bf16[4,8,2,192,256]{4,3,2,1,0:T(8,128)(2,1)}, u32[]{:S(2)}) copy-start(bf16[4,8,2,192,256]{4,3,2,1,0:T(8,128)(2,1)} %shard_map.120) | copy-start | bytes 18874372
  163.2 13.4 %copy-start.1 = (bf16[4096,512]{1,0:T(8,128)(2,1)S(1)}, bf16[4096,512]{1,0:T(8,128)(2,1)}, u32[]{:S(2)}) copy-start(bf16[4096,512]{1,0:T(8,128)(2,1)} %slice.61) | copy-start | bytes 12582916

commit v2 on v0

v2 whole, which is shorter than its diff:
```python
import functools
import math

import jax
import jax.numpy as jnp
from jax import lax
from jax.experimental import pallas as pl
from jax.experimental.pallas import tpu as pltpu
from jax.sharding import PartitionSpec as P

D = 4096
HD = 128
NX, NY, NC, NZ = 4, 8, 2, 8
MESH = pl.DeviceIdType.MESH

EPSILON = 1e-05
ROPE_BASE = 1000000.0
NEG_FILL = -1e30


def place():
    s = lax.axis_index("seq")
    return s // (NY * NC), (s // NC) % NY, s % NC


def seq_of(x, y, c):
    return ((x % NX) * NY + y % NY) * NC + c


class Sends:
    def __init__(self, send_sems, recv_sems):
        self.send_sems, self.recv_sems, self.made = send_sems, recv_sems, []

    def start(self, src, dst, device_id):
        at = len(self.made)
        copy = pltpu.make_async_remote_copy(
            src_ref=src,
            dst_ref=dst,
            send_sem=self.send_sems.at[at],
            recv_sem=self.recv_sems.at[at],
            device_id=device_id,
            device_id_type=MESH,
        )
        copy.start()
        self.made.append(copy)
        return copy

    def finish(self):
        for copy in self.made:
            copy.wait_send()


def wait_all(copies):
    for copy in copies:
        copy.wait_recv()


def ring_near(n, block, source, to, sends):
    return [sends.start(source, block(0), to(d)) for d in (2, -2, 1, -1)]


def ring_far(at, block, to, sends):
    odd = at % 2
    return [
        sends.start(block(-2), block(-2), to(1)),
        sends.start(block(2), block(2), to(-1)),
        sends.start(block(4 * odd - 2), block(4 * odd - 2), to(2 - 4 * odd)),
    ]


NEAR = (-2, 2, -1, 1)
FAR = (-3, 3, 4)


def plane_steps(src, out, sends, local_sem, split):
    x, y, c = place()
    a_rows, b_rows = pl.ds(0, split), pl.ds(split, src.shape[0] - split)
    every_x = pl.ds(0, NX)
    right = {"seq": seq_of(x + 1, y, c)}
    left = {"seq": seq_of(x + NX - 1, y, c)}
    other = {"seq": seq_of(x, y, 1 - c)}

    def col(k):
        return (y + k + NY) % NY

    def up(k):
        return {"seq": seq_of(x, y + k + NY, c)}

    def a_block(k):
        return out.at[every_x, col(k), c, a_rows]

    def b_block(k, xx=x):
        return out.at[xx, col(k), c, b_rows]

    def spread(k, source=None):
        source = b_block(k) if source is None else source
        return [sends.start(source, b_block(k), right), sends.start(source, b_block(k), left)]

    def forward(k):
        odd = col(k) % 2
        block = b_block(k, (x + NX - 1 + 2 * odd) % NX)
        return sends.start(block, block, {"seq": seq_of(x + 1 + 2 * odd, y, c)})

    handed = []

    def hand(ref):
        handed.append(sends.start(ref, ref, other))

    own = pltpu.make_async_copy(src, out.at[x, y, c], local_sem)
    own.start()
    ring_b = ring_near(NY, b_block, src.at[b_rows], up, sends)
    if split:
        along = [
            sends.start(src.at[a_rows], out.at[x, y, c, a_rows], {"seq": seq_of(x + d, y, c)})
            for d in (2, 1, 3)
        ]
    own_spread = spread(0, src.at[b_rows])
    yield
    own.wait()
    if split:
        wait_all(along)
        ring_a = ring_near(NY, a_block, a_block(0), up, sends)
    wait_all(ring_b)
    ring_b = ring_far(y, b_block, up, sends)
    near_spread = [spread(k) for k in NEAR]
    if split:
        hand(a_block(0))
    wait_all(own_spread)
    own_forward = forward(0)
    yield
    if split:
        wait_all(ring_a)
        ring_a = ring_far(y, a_block, up, sends)
    wait_all(ring_b)
    far_spread = [spread(k) for k in FAR]
    near_forward = []
    for k, copies in zip(NEAR, near_spread):
        wait_all(copies)
        near_forward.append(forward(k))
    if split:
        for k in NEAR:
            hand(a_block(k))
    wait_all([own_forward])
    hand(b_block(0, every_x))
    yield
    far_forward = []
    for k, copies in zip(FAR, far_spread):
        wait_all(copies)
        far_forward.append(forward(k))
    if split:
        wait_all(ring_a)
        for k in FAR:
            hand(a_block(k))
    for k, copy in zip(NEAR, near_forward):
        wait_all([copy])
        hand(b_block(k, every_x))
    yield
    for k, copy in zip(FAR, far_forward):
        wait_all([copy])
        hand(b_block(k, every_x))
    yield
    wait_all(handed)


def line_steps(src, out, sends, local_sem):
    z = lax.axis_index("head")

    def to(k):
        return {"head": (z + k + NZ) % NZ}

    def block(k):
        return out.at[(z + k + NZ) % NZ]

    own = pltpu.make_async_copy(src, block(0), local_sem)
    own.start()
    ring = ring_near(NZ, block, src, to, sends)
    own.wait()
    yield
    wait_all(ring)
    ring = ring_far(z, block, to, sends)
    yield
    wait_all(ring)


def greet():
    x, y, c = place()
    z = lax.axis_index("head")
    partners = [{"seq": seq_of(x + d, y, c)} for d in (1, 2, 3)]
    partners += [{"seq": seq_of(x, y + d, c)} for d in (1, 2, NY - 2, NY - 1)]
    partners += [{"seq": seq_of(x, y, 1 - c)}]
    partners += [{"head": (z + d) % NZ} for d in range(1, NZ)]
    barrier = pltpu.get_barrier_semaphore()
    for partner in partners:
        pl.semaphore_signal(barrier, inc=1, device_id=partner, device_id_type=MESH)
    pl.semaphore_wait(barrier, len(partners))


PIC_COPIES = 39
PLANE_COPIES = 57
LINE_COPIES = 7


def advance(*runs):
    for run in runs:
        next(run, None)


def block_kernel(
    dims,
    pics,
    text,
    rec,
    w_in,
    w_out,
    gain,
    cosine,
    sine,
    cache,
    chosen,
    out,
    pics_all,
    raw,
    raw_all,
    w_in_all,
    w_out_all,
    kv_own,
    kv_all,
    queries,
    best,
    total,
    accum,
    attended,
    parts,
    arrived,
    send_sems,
    recv_sems,
    local_sems,
):
    tok, width, rec_count, cache_rows, group = dims
    s = lax.axis_index("seq")
    z = lax.axis_index("head")
    greet()
    sends = Sends(send_sems, recv_sems)
    pic_run = plane_steps(pics, pics_all, sends, local_sems.at[0], 0)
    in_run = plane_steps(w_in, w_in_all, sends, local_sems.at[1], 16)
    out_run = plane_steps(w_out, w_out_all, sends, local_sems.at[2], 16)
    advance(pic_run, pic_run, in_run, pic_run, pic_run, in_run, pic_run, out_run, pic_run)

    pictures = pics_all[...].reshape(-1, pics.shape[1])
    slot = pictures[:, width : width + 1].astype(jnp.float32) * HD + pictures[
        :, width + 1 : width + 2
    ].astype(jnp.float32)
    position = (s * tok + lax.broadcasted_iota(jnp.int32, (1, tok), 1)).astype(jnp.float32)
    select = (slot == position).astype(jnp.float32).astype(jnp.bfloat16)
    placed = lax.dot_general(
        select, pictures, (((0,), (0,)), ((), ())), preferred_element_type=jnp.float32
    )
    hit = placed[:, width + 2 : width + 3] > 0.5
    raw[:tok, :] = jnp.where(hit, placed[:, :width], text[...].astype(jnp.float32)).astype(
        jnp.bfloat16
    )
    raw[tok:, :] = rec[...]
    line_run = line_steps(raw, raw_all, sends, local_sems.at[3])
    advance(line_run, in_run, out_run, line_run, in_run, out_run, in_run, line_run)

    rows = raw.shape[0]
    squares = jnp.zeros((rows, 1), jnp.float32)
    for zz in range(NZ):
        wide = raw_all[zz].astype(jnp.float32)
        squares = squares + jnp.sum(wide * wide, axis=1, keepdims=True)
    shrink = lax.rsqrt(squares / D + EPSILON)
    advance(in_run, out_run)
    projected = jnp.zeros((rows, w_in.shape[1]), jnp.float32)
    half = NY // 2
    for zz in range(NZ):
        normed = (
            raw_all[zz].astype(jnp.float32) * shrink * gain[:, zz * width : (zz + 1) * width]
        ).astype(jnp.bfloat16)
        block = w_in_all[zz // 2, half * (zz % 2) : half * (zz % 2 + 1)].reshape(width, -1)
        projected = projected + jnp.dot(normed, block, preferred_element_type=jnp.float32)

    def rotated(at):
        values = projected[:, at * HD : (at + 1) * HD]
        return values * cosine[...] + pltpu.roll(values, HD // 2, 1) * sine[...]

    for g in range(group):
        queries[g * tok : (g + 1) * tok, :] = rotated(g)[:tok].astype(jnp.bfloat16)
    pair = jnp.concatenate([rotated(group), projected[:, (group + 1) * HD :]], axis=1)
    kv_own[cache_rows:, :] = pair[:tok].astype(jnp.bfloat16)
    fresh = pair[tok:].astype(jnp.bfloat16).astype(jnp.float32)
    kept = cache[...].astype(jnp.float32)
    for r in range(rec_count):
        kept = jnp.where(chosen[:, r : r + 1] > 0.5, fresh[r : r + 1, :], kept)
    kv_own[:cache_rows, :] = kept.astype(jnp.bfloat16)
    kv_run = plane_steps(kv_own, kv_all, sends, local_sems.at[4], 48)
    advance(kv_run, out_run, kv_run, out_run, kv_run, kv_run, kv_run, kv_run)

    best[...] = jnp.full_like(best, NEG_FILL)
    total[...] = jnp.zeros_like(total)
    accum[...] = jnp.zeros_like(accum)
    scale = HD**-0.5 * math.log2(math.e)
    kv_rows = cache_rows + tok
    span = half * NC

    def update(block, mask):
        keys, values = block[:, :HD], block[:, HD:]
        scores = lax.dot_general(
            queries[...], keys, (((1,), (1,)), ((), ())), preferred_element_type=jnp.float32
        )
        if mask is not None:
            scores = jnp.where(mask, scores, NEG_FILL)
        old = best[...]
        top = jnp.maximum(old, jnp.max(scores, axis=1, keepdims=True))
        factor = jnp.exp2((old - top) * scale)
        weights = jnp.exp2((scores - top) * scale)
        best[...] = top
        total[...] = total[...] * factor + jnp.sum(weights, axis=1, keepdims=True)
        accum[...] = accum[...] * factor + jnp.dot(
            weights.astype(jnp.bfloat16), values, preferred_element_type=jnp.float32
        )

    def visit(step, carry):
        xx, y0 = step // 2, half * (step % 2)

        @pl.when(step < s // span)
        def _():
            update(kv_all[xx, pl.ds(y0, half)].reshape(span * kv_rows, 2 * HD), None)

        @pl.when(step == s // span)
        def _():
            at = lax.broadcasted_iota(jnp.int32, (1, span * kv_rows), 1)
            row = at % kv_rows
            key_pos = jnp.where(
                row < cache_rows, -1, (step * span + at // kv_rows) * tok + row - cache_rows
            )
            query_pos = s * tok + lax.broadcasted_iota(jnp.int32, (group * tok, 1), 0) % tok
            update(
                kv_all[xx, pl.ds(y0, half)].reshape(span * kv_rows, 2 * HD), key_pos <= query_pos
            )

        @pl.when(step > s // span)
        def _():
            update(
                kv_all[xx, pl.ds(y0, half), :, pl.ds(0, cache_rows), :].reshape(
                    span * cache_rows, 2 * HD
                ),
                None,
            )

        return carry

    lax.fori_loop(0, NX * 2, visit, 0)
    result = accum[...] / total[...]
    for g in range(group):
        attended[:, g * HD : (g + 1) * HD] = result[g * tok : (g + 1) * tok].astype(jnp.bfloat16)
    advance(out_run)

    def columns(d):
        zz = (z + d) % NZ
        block = w_out_all[zz // 2, pl.ds(half * (zz % 2), half)].reshape(width, -1)
        return lax.dot_general(
            attended[...], block, (((1,), (1,)), ((), ())), preferred_element_type=jnp.float32
        )

    shares = []
    for d in (4, 3, 5, 2, 6, 1, 7):
        parts[d] = columns(d).astype(jnp.bfloat16)
        shares.append(sends.start(parts.at[d], arrived.at[d], {"head": (z + d) % NZ}))
    mixed = columns(0)
    wait_all(shares)
    for d in range(1, NZ):
        mixed = mixed + arrived[d].astype(jnp.float32)
    out[...] = mixed.astype(jnp.bfloat16)
    sends.finish()


def on_device(
    text_rows,
    picture_rows,
    picture_slots,
    norm_gain,
    w_query,
    w_key,
    w_value,
    w_out,
    cache_keys,
    cache_values,
    recompute_rows,
    recompute_slots,
):
    tok, width = text_rows.shape
    rec_count = recompute_rows.shape[0]
    cache_rows = cache_keys.shape[0]
    group = w_query.shape[1] // HD
    rec_rows = 16
    seq_index = lax.axis_index("seq")
    marks = jnp.stack(
        [picture_slots // HD, picture_slots % HD, jnp.ones_like(picture_slots)], axis=1
    ).astype(jnp.bfloat16)
    pics = jnp.concatenate([picture_rows, jnp.pad(marks, ((0, 0), (0, HD - 3)))], axis=1)
    rec = jnp.pad(recompute_rows, ((0, rec_rows - rec_count), (0, 0)))
    w_in = jnp.concatenate([w_query, w_key, w_value], axis=1)
    cache = jnp.concatenate([cache_keys, cache_values], axis=1)
    chosen = (
        (recompute_slots - seq_index * cache_rows)[None, :]
        == jnp.arange(cache_rows, dtype=jnp.int32)[:, None]
    ).astype(jnp.float32)
    positions = jnp.concatenate(
        [
            cache_rows * lax.axis_size("seq") + seq_index * tok + jnp.arange(tok, dtype=jnp.int32),
            jnp.pad(recompute_slots, (0, rec_rows - rec_count)),
        ]
    ).astype(jnp.float32)
    freqs = ROPE_BASE ** (-jnp.arange(HD // 2, dtype=jnp.float32) / (HD // 2))
    angles = positions[:, None] * freqs[None, :]
    cosine, sine = jnp.cos(angles), jnp.sin(angles)
    rows = tok + rec_rows
    kv_rows = cache_rows + tok
    plane = (NX, NY, NC)
    bf16, f32 = jnp.bfloat16, jnp.float32
    copies = PIC_COPIES + 3 * PLANE_COPIES + 2 * LINE_COPIES
    vmem = pl.BlockSpec(memory_space=pltpu.VMEM)
    operands = (
        pics,
        text_rows,
        rec,
        w_in,
        w_out.T,
        norm_gain[None, :],
        jnp.concatenate([cosine, cosine], axis=1),
        jnp.concatenate([-sine, sine], axis=1),
        cache,
        chosen,
    )
    return pl.pallas_call(
        functools.partial(block_kernel, (tok, width, rec_count, cache_rows, group)),
        out_shape=jax.ShapeDtypeStruct((tok, width), bf16),
        in_specs=[vmem] * len(operands),
        out_specs=vmem,
        scratch_shapes=[
            pltpu.VMEM(plane + pics.shape, bf16),
            pltpu.VMEM((rows, width), bf16),
            pltpu.VMEM((NZ, rows, width), bf16),
            pltpu.VMEM(plane + w_in.shape, bf16),
            pltpu.VMEM(plane + w_out.shape[::-1], bf16),
            pltpu.VMEM((kv_rows, 2 * HD), bf16),
            pltpu.VMEM(plane + (kv_rows, 2 * HD), bf16),
            pltpu.VMEM((group * tok, HD), bf16),
            pltpu.VMEM((group * tok, 1), f32),
            pltpu.VMEM((group * tok, 1), f32),
            pltpu.VMEM((group * tok, HD), f32),
            pltpu.VMEM((tok, group * HD), bf16),
            pltpu.VMEM((NZ, tok, width), bf16),
            pltpu.VMEM((NZ, tok, width), bf16),
            pltpu.SemaphoreType.DMA((copies,)),
            pltpu.SemaphoreType.DMA((copies,)),
            pltpu.SemaphoreType.DMA((5,)),
        ],
        compiler_params=pltpu.CompilerParams(
            collective_id=0, has_side_effects=True, vmem_limit_bytes=56 * 1024 * 1024
        ),
    )(*operands)


def solution(mesh):
    return jax.shard_map(
        on_device,
        mesh=mesh,
        in_specs=(
            P("seq", "head"),
            P("seq", "head"),
            P("seq"),
            P(),
            P("seq", "head"),
            P("seq", "head"),
            P("seq", "head"),
            P("head", "seq"),
            P("seq", "head"),
            P("seq", "head"),
            P("seq", "head"),
            P("seq"),
        ),
        out_specs=P("seq", "head"),
        check_vma=False,
    )
```

time: 878 us -> 145 us (0.17)
  waiting for transfers between devices: 751 us -> 0 us
  Pallas kernels: 0 us -> 136 us
  blocking collectives: 48.6 us -> 0 us
  matrix products: 41.5 us -> 0 us
  between operations: 14.1 us -> 0.04 us
    all_gather x10 -> x0, waiting for transfers between devices: 712 us -> none  [the longest x1 85.8 us: on_device(): lax.all_gather(w_key, 'seq', axis=0, tiled=True)]
    pallas_call x0 -> x1, Pallas kernels: none -> 136 us  [on_device(): pl.pallas_call(functools.partial(block_kernel, (tok, width, rec_count, ca...]
    dot_general x11 -> x0, matrix products: 41.5 us -> none  [the longest x2 15.3 us: attend(): jnp.einsum('kgtn,nkd->kgtd', weights.astype(jnp.bfloat16), values_split,...]
    reduce_scatter x1 -> x0, waiting for transfers between devices: 36.4 us -> none  [on_device(): lax.psum_scatter(partial_out.astype(jnp.bfloat16), 'head', scatter_dimens...]
    all_gather x1 -> x0, blocking collectives: 18.7 us -> none  [on_device(): lax.all_gather(scaled(rec_wide, rec_sq, gain_slice), 'head', axis=1, tile...]
    unnamed x1 -> x0, blocking collectives: 15.5 us -> none
    psum x1 -> x0, blocking collectives: 14.4 us -> none  [on_device(): lax.psum((jnp.sum(stream_wide * stream_wide, axis=1), jnp.sum(rec_wide *...]
  transfers between devices with their start and end apart: 11 -> 0, of which waited for: 11 -> 0; matrix products, arithmetic and copies ran while one was open for 6% -> 0% of each run, Pallas kernels for 0% -> 0%
where the time goes in v2:
time: 145 us; the launch traced here: 144 us
  Pallas kernels  136 us (94%)
  local copies, waits for them, and re-layouts  3.95 us (3%)
  other arithmetic  3.72 us (3%)
    pallas_call x1, Pallas kernels, on_device(): pl.pallas_call(functools.partial(block_kernel, (tok, width, rec_count, ca...  136 us
    unnamed x19, local copies, waits for them, and re-layouts  3.17 us

profile of v2, /device:TPU:7, one launch (start us, length us, event | category | flops | bytes accessed | tf_op | source)
XLA Modules:
  0.0 144.0 jit_solution(8831964196809198447)
XLA Ops:
  0.0 0.0 copy-start.7
  0.0 0.6 copy-done.7
  0.7 0.3 fusion.3
  1.0 0.0 copy-start.1
  1.0 0.8 pad_maximum_fusion.1
  1.8 0.0 copy-start.8
  1.8 0.7 copy-done.8
  2.5 0.1 pad.30.clone
  2.5 0.0 copy-start
  2.5 0.1 maximum_maximum_fusion
  2.6 0.1 copy.15
  2.7 0.0 copy-done.1
  2.7 0.6 fusion.1.pics
  3.4 0.0 copy-start.2
  3.4 0.0 copy-start.3
  3.4 0.6 fusion.2.chosen
  4.0 0.0 copy-done
  4.0 0.1 copy-done.2
  4.1 0.0 copy-done.3
  4.1 0.0 copy-start.4
  4.1 0.0 copy-start.5
  4.1 0.6 pad_maximum_fusion.w_in
  4.8 0.1 copy-done.4
  4.8 0.0 copy-done.5
  4.8 0.0 copy-start.6
  4.8 0.6 pad_maximum_fusion.3.cache
  5.5 0.1 copy-done.6
  5.5 0.6 pad.13.rec
  6.1 136.3 %shard_map.118 = bf16[128,512]{1,0:T(8,128)(2,1)} custom-call(bf16[32,640]{1,0:T(8,128)(2,1)} %fusion.1.pics, bf16[128,512]{1,0:T(8,128)(2,1)} %text.1, bf16[16,512]{1,0:T(8,128)(2,1)} %pad.13.rec, bf16[64,768]{1,0:T(8,128)(2,1)} %pad_maximum_fusion.w_in, bf16[64,512]{1,0:T(8,128)(2,1)} %bitcast.7, f32[1,4096]{1,0:T(1,128)} %bitcast.8, ...), custom_call_target="tpu_custom_call" | custom-call | tf_op jit(solution)/shard_map/pallas_call | solution.py:435
  142.4 1.6 %copy.17 = bf16[128,512]{1,0:T(8,128)(2,1)} copy(bf16[128,512]{1,0:T(8,128)(2,1)} %shard_map.118) | data formatting | bytes 262144
  (5 shorter events, 0.0 us)
Async XLA Ops:
  0.0 0.7 copy-start.7
  1.0 1.7 %copy-start.1 = (bf16[32,512]{1,0:T(8,128)(2,1)S(1)}, bf16[32,512]{1,0:T(8,128)(2,1)}, u32[]{:S(2)}) copy-start(bf16[32,512]{1,0:T(8,128)(2,1)} %param.13) | copy-start | bytes 98308
  1.8 0.7 copy-start.8
  2.5 1.4 copy-start
  3.4 0.7 copy-start.2
  3.4 0.8 copy-start.3
  4.1 0.7 copy-start.4
  4.1 0.7 copy-start.5
  4.8 0.7 copy-start.6

commit v3 on v2

v3 whole, which is shorter than its diff:
```python
import functools
import math

import jax
import jax.numpy as jnp
import numpy as np
from jax import lax
from jax.experimental import pallas as pl
from jax.experimental.pallas import tpu as pltpu
from jax.sharding import PartitionSpec as P

D = 4096
HD = 128
NX, NY, NC, NZ = 4, 8, 2, 8
MESH = pl.DeviceIdType.MESH

EPSILON = 1e-05
ROPE_BASE = 1000000.0
NEG_FILL = -1e30
ABSENT = 2.0**127


def place():
    s = lax.axis_index("seq")
    return s // (NY * NC), (s // NC) % NY, s % NC


def seq_of(x, y, c):
    return ((x % NX) * NY + y % NY) * NC + c


class Sends:
    def __init__(self, send_sems, recv_sems):
        self.send_sems, self.recv_sems, self.made = send_sems, recv_sems, []

    def start(self, src, dst, device_id):
        at = len(self.made)
        copy = pltpu.make_async_remote_copy(
            src_ref=src,
            dst_ref=dst,
            send_sem=self.send_sems.at[at],
            recv_sem=self.recv_sems.at[at],
            device_id=device_id,
            device_id_type=MESH,
        )
        copy.start()
        self.made.append(copy)
        return copy

    def finish(self):
        for copy in self.made:
            copy.wait_send()


def wait_all(copies):
    for copy in copies:
        copy.wait_recv()


def ring_near(n, block, source, to, sends):
    return [sends.start(source, block(0), to(d)) for d in (2, -2, 1, -1)]


def ring_far(at, block, to, sends):
    odd = at % 2
    return [
        sends.start(block(-2), block(-2), to(1)),
        sends.start(block(2), block(2), to(-1)),
        sends.start(block(4 * odd - 2), block(4 * odd - 2), to(2 - 4 * odd)),
    ]


NEAR = (-2, 2, -1, 1)
FAR = (-3, 3, 4)


def plane_steps(src, out, sends, local_sem, split):
    x, y, c = place()
    a_rows, b_rows = pl.ds(0, split), pl.ds(split, src.shape[0] - split)
    every_x = pl.ds(0, NX)
    right = {"seq": seq_of(x + 1, y, c)}
    left = {"seq": seq_of(x + NX - 1, y, c)}
    other = {"seq": seq_of(x, y, 1 - c)}

    def col(k):
        return (y + k + NY) % NY

    def up(k):
        return {"seq": seq_of(x, y + k + NY, c)}

    def a_block(k):
        return out.at[every_x, col(k), c, a_rows]

    def b_block(k, xx=x):
        return out.at[xx, col(k), c, b_rows]

    def spread(k, source=None):
        source = b_block(k) if source is None else source
        return [sends.start(source, b_block(k), right), sends.start(source, b_block(k), left)]

    def forward(k):
        odd = col(k) % 2
        block = b_block(k, (x + NX - 1 + 2 * odd) % NX)
        return sends.start(block, block, {"seq": seq_of(x + 1 + 2 * odd, y, c)})

    handed = []

    def hand(ref):
        handed.append(sends.start(ref, ref, other))

    own = pltpu.make_async_copy(src, out.at[x, y, c], local_sem)
    own.start()
    ring_b = ring_near(NY, b_block, src.at[b_rows], up, sends)
    if split:
        along = [
            sends.start(src.at[a_rows], out.at[x, y, c, a_rows], {"seq": seq_of(x + d, y, c)})
            for d in (2, 1, 3)
        ]
    own_spread = spread(0, src.at[b_rows])
    yield
    own.wait()
    if split:
        wait_all(along)
        ring_a = ring_near(NY, a_block, a_block(0), up, sends)
    wait_all(ring_b)
    ring_b = ring_far(y, b_block, up, sends)
    near_spread = [spread(k) for k in NEAR]
    if split:
        hand(a_block(0))
    wait_all(own_spread)
    own_forward = forward(0)
    yield
    if split:
        wait_all(ring_a)
        ring_a = ring_far(y, a_block, up, sends)
    wait_all(ring_b)
    far_spread = [spread(k) for k in FAR]
    near_forward = []
    for k, copies in zip(NEAR, near_spread):
        wait_all(copies)
        near_forward.append(forward(k))
    if split:
        for k in NEAR:
            hand(a_block(k))
    wait_all([own_forward])
    hand(b_block(0, every_x))
    yield
    far_forward = []
    for k, copies in zip(FAR, far_spread):
        wait_all(copies)
        far_forward.append(forward(k))
    if split:
        wait_all(ring_a)
        for k in FAR:
            hand(a_block(k))
    for k, copy in zip(NEAR, near_forward):
        wait_all([copy])
        hand(b_block(k, every_x))
    yield
    for k, copy in zip(FAR, far_forward):
        wait_all([copy])
        hand(b_block(k, every_x))
    yield
    wait_all(handed)


def line_steps(src, out, sends, local_sem, seen):
    z = lax.axis_index("head")
    odd = z % 2
    up, down = {"head": (z + 1) % NZ}, {"head": (z + NZ - 1) % NZ}

    def block(k):
        return out.at[(z + k + NZ) % NZ]

    own = pltpu.make_async_copy(src, block(0), local_sem)
    own.start()
    ring = [sends.start(src, block(0), up), sends.start(src, block(0), down)]
    own.wait()
    seen(z)
    yield
    for k in range(1, NZ // 2):
        wait_all(ring)
        if k < NZ // 2 - 1:
            ring = [
                sends.start(block(-k), block(-k), up),
                sends.start(block(k), block(k), down),
            ]
        else:
            far = block(k * (2 * odd - 1))
            ring = [sends.start(far, far, {"head": (z + 1 + odd * (NZ - 2)) % NZ})]
        seen((z - k + NZ) % NZ)
        seen((z + k) % NZ)
        yield
    wait_all(ring)
    seen((z + NZ // 2) % NZ)


def greet():
    x, y, c = place()
    z = lax.axis_index("head")
    partners = [{"seq": seq_of(x + d, y, c)} for d in (1, 2, 3)]
    partners += [{"seq": seq_of(x, y + d, c)} for d in (1, 2, NY - 2, NY - 1)]
    partners += [{"seq": seq_of(x, y, 1 - c)}]
    partners += [{"head": (z + d) % NZ} for d in range(1, NZ)]
    barrier = pltpu.get_barrier_semaphore()
    for partner in partners:
        pl.semaphore_signal(barrier, inc=1, device_id=partner, device_id_type=MESH)
    pl.semaphore_wait(barrier, len(partners))


START = "p"
PLACING = "pipipcpip"
LINING = "iclo" "ilci" "locl"
NORMING = "co"
KEYING = ("c", "ko", "ko", "ko", "kko")

PIC_COPIES = 39
PLANE_COPIES = 57
LINE_COPIES = 7


def advance(*runs):
    for run in runs:
        next(run, None)


def drain(run):
    for _ in run:
        pass


def block_kernel(dims, *refs):
    tok, width, rec_count, cache_rows, group = dims
    operands, refs = refs[:13], refs[13:]
    hbm_in = operands[:9]
    gain, freqs, slots, rec_slots = operands[9:]
    out, refs = refs[0], refs[1:]
    pics, text, rec, w_in, w_out, cache = refs[:6]
    turns, cache_own, raw, kv_own = refs[6:10]
    pics_all, raw_all, w_in_all, w_out_all, cache_all, kv_all = refs[10:16]
    squares, queries, best, accum, attended = refs[16:21]
    parts, sums, relayed, arrived = refs[21:25]
    send_sems, recv_sems, local_sems, load_sems = refs[25:]

    s = lax.axis_index("seq")
    z = lax.axis_index("head")
    key_cols = HD
    query_cols = group * HD
    places = (
        pics.at[:, pl.ds(0, width)],
        text,
        rec,
        w_in.at[:, pl.ds(0, query_cols)],
        w_in.at[:, pl.ds(query_cols, key_cols)],
        w_in.at[:, pl.ds(query_cols + key_cols, key_cols)],
        w_out,
        cache.at[:, pl.ds(0, key_cols)],
        cache.at[:, pl.ds(key_cols, key_cols)],
    )
    loads = [
        pltpu.make_async_copy(given, here, load_sems.at[i])
        for i, (given, here) in enumerate(zip(hbm_in, places))
    ]
    for load in loads:
        load.start()

    def column(values, count):
        shape = (count, values.shape[1])
        row = lax.broadcasted_iota(jnp.int32, shape, 0)
        lane = lax.broadcasted_iota(jnp.int32, shape, 1)
        return jnp.sum(jnp.where(row == lane, values, 0), axis=1, keepdims=True)

    at_stream = column(slots[...], pics.shape[0])
    lane = lax.broadcasted_iota(jnp.int32, (pics.shape[0], HD), 1)
    marks = jnp.where(lane == 0, at_stream // HD, jnp.where(lane == 1, at_stream % HD, 1))
    pics[:, width:] = marks.astype(jnp.float32).astype(jnp.bfloat16)
    greet()
    for load in loads:
        load.wait()
    sends = Sends(send_sems, recv_sems)
    pic_run = plane_steps(pics, pics_all, sends, local_sems.at[0], 0)
    in_run = plane_steps(w_in, w_in_all, sends, local_sems.at[1], 16)
    out_run = plane_steps(w_out, w_out_all, sends, local_sems.at[2], 16)
    cache_run = plane_steps(cache_own, cache_all, sends, local_sems.at[3], 16)
    runs = {"p": pic_run, "i": in_run, "o": out_run, "c": cache_run}

    def go(order):
        for name in order:
            advance(*(runs[name] if name == "l" else [runs[name]]))

    go(START)

    cache_at = lax.broadcasted_iota(jnp.int32, (cache_rows, rec_count), 0) + s * cache_rows
    chosen = (cache_at == rec_slots[...]).astype(jnp.float32)
    gone = jnp.max(chosen, axis=1, keepdims=True) > 0.5
    kept_keys = cache[:, :HD].astype(jnp.float32)
    repeat = kept_keys[rec_count : rec_count + 1]
    for r in range(rec_count - 1, -1, -1):
        repeat = jnp.where(gone[r : r + 1], repeat, kept_keys[r : r + 1])
    cache_own[:, :HD] = jnp.where(gone, repeat, kept_keys).astype(jnp.bfloat16)
    cache_own[:, HD:] = jnp.where(gone, ABSENT, cache[:, HD:].astype(jnp.float32)).astype(
        jnp.bfloat16
    )

    rows = raw.shape[1]
    lane = lax.broadcasted_iota(jnp.int32, (1, HD), 1)
    stream_at = lax.broadcasted_iota(jnp.int32, (tok, 1), 0) + (s * tok + NX * NY * NC * cache_rows)
    for first, place_of in ((0, stream_at), (tok, column(rec_slots[...], rows - tok))):
        angles = place_of.astype(jnp.float32) * freqs[...]
        sine = jnp.sin(angles)
        last = first + angles.shape[0]
        turns[first:last, :HD] = jnp.cos(angles)
        turns[first:last, HD:] = jnp.where(lane < HD // 2, -sine, sine)
    go(PLACING)
    drain(pic_run)

    pictures = pics_all[...].reshape(-1, pics.shape[1])
    slot = pictures[:, width : width + 1].astype(jnp.float32) * HD + pictures[
        :, width + 1 : width + 2
    ].astype(jnp.float32)
    position = (s * tok + lax.broadcasted_iota(jnp.int32, (1, tok), 1)).astype(jnp.float32)
    select = (slot == position).astype(jnp.float32).astype(jnp.bfloat16)
    placed = lax.dot_general(
        select, pictures, (((0,), (0,)), ((), ())), preferred_element_type=jnp.float32
    )
    hit = placed[:, width + 2 : width + 3] > 0.5
    stream = jnp.where(hit, placed[:, :width], text[...].astype(jnp.float32)).astype(jnp.bfloat16)
    part = width // 2
    extra = jnp.concatenate(
        [
            rec[...].astype(jnp.float32),
            jnp.zeros((rows - tok - rec_count, width), jnp.float32),
        ],
        axis=0,
    ).astype(jnp.bfloat16)
    squares[...] = jnp.zeros_like(squares)

    def line(j):
        def seen(at):
            wide = raw_all[j, at].astype(jnp.float32)
            squares[...] += jnp.sum(wide * wide, axis=1, keepdims=True)

        return line_steps(raw.at[j], raw_all.at[j], sends, local_sems.at[4 + j], seen)

    lines = [line(j) for j in range(2)]
    runs["l"] = lines
    for j in range(2):
        raw[j, :tok, :] = stream[:, j * part : (j + 1) * part]
        raw[j, tok:, :] = extra[:, j * part : (j + 1) * part]
        advance(lines[j])
    go(LINING)
    drain(lines[0])
    drain(lines[1])

    shrink = lax.rsqrt(squares[...] / D + EPSILON)
    go(NORMING)
    drain(in_run)
    projected = jnp.zeros((rows, w_in.shape[1]), jnp.float32)
    half = NY // 2
    quarter = half // 2
    for zz in range(NZ):
        for j in range(2):
            at = zz * width + j * part
            normed = (raw_all[j, zz].astype(jnp.float32) * shrink * gain[:, at : at + part]).astype(
                jnp.bfloat16
            )
            y0 = half * (zz % 2) + quarter * j
            block = w_in_all[zz // 2, y0 : y0 + quarter].reshape(part, -1)
            projected = projected + jnp.dot(normed, block, preferred_element_type=jnp.float32)

    def rotated(at):
        values = projected[:, at * HD : (at + 1) * HD]
        return values * turns[:, :HD] + pltpu.roll(values, HD // 2, 1) * turns[:, HD:]

    pair = jnp.concatenate([rotated(group), projected[:, (group + 1) * HD :]], axis=1)
    kv_own[:tok, :] = pair[:tok].astype(jnp.bfloat16)
    fresh = pair[tok:]
    valid = lax.broadcasted_iota(jnp.int32, (rows - tok, 1), 0) < rec_count
    kv_own[tok:, :HD] = jnp.where(valid, fresh[:, :HD], fresh[:1, :HD]).astype(jnp.bfloat16)
    kv_own[tok:, HD:] = jnp.where(valid, fresh[:, HD:], ABSENT).astype(jnp.bfloat16)
    kv_run = plane_steps(kv_own, kv_all, sends, local_sems.at[6], 32)
    advance(kv_run)
    runs["k"] = kv_run
    go(KEYING[0])
    drain(cache_run)

    scale = HD**-0.5 * math.log2(math.e)
    few = tok // 2
    for g in range(group):
        turned = (rotated(g) * scale).astype(jnp.bfloat16)
        for h in range(2):
            queries[h, g * few : (g + 1) * few, :] = turned[h * few : (h + 1) * few]
    best[...] = jnp.full_like(best, NEG_FILL)
    accum[...] = jnp.zeros_like(accum)
    span = half * NC

    def update(h, block, mask):
        keys = block[:, :HD]
        values = block[:, HD:].astype(jnp.float32)
        present = values < ABSENT / 2
        values = jnp.concatenate(
            [jnp.where(present, values, 0.0), jnp.where(present, 1.0, 0.0)], axis=1
        ).astype(jnp.bfloat16)
        scores = lax.dot_general(
            queries[h], keys, (((1,), (1,)), ((), ())), preferred_element_type=jnp.float32
        )
        if mask is not None:
            scores = jnp.where(mask, scores, NEG_FILL)
        old = best[h]
        top = jnp.maximum(old, jnp.max(scores, axis=1, keepdims=True))
        factor = jnp.exp2(old - top)
        weights = jnp.exp2(scores - top).astype(jnp.bfloat16)
        best[h] = top
        accum[h] = accum[h] * factor + jnp.dot(weights, values, preferred_element_type=jnp.float32)

    def visit_cache(first, last):
        def visit(step, carry):
            block = cache_all[step // 2, pl.ds(half * (step % 2), half)]
            block = block.reshape(span * cache_rows, 2 * HD)
            for h in range(2):
                update(h, block, None)
            return carry

        lax.fori_loop(first, last, visit, 0)

    def visit_new(h):
        def visit(step, carry):
            xx, y0 = step // 2, half * (step % 2)

            @pl.when(step < s // span)
            def _():
                update(h, kv_all[xx, pl.ds(y0, half)].reshape(span * rows, 2 * HD), None)

            @pl.when(step == s // span)
            def _():
                at = lax.broadcasted_iota(jnp.int32, (1, span * rows), 1)
                row = at % rows
                key_pos = jnp.where(row < tok, (step * span + at // rows) * tok + row, -1)
                query_at = lax.broadcasted_iota(jnp.int32, (group * few, 1), 0)
                query_pos = s * tok + h * few + query_at % few
                update(
                    h,
                    kv_all[xx, pl.ds(y0, half)].reshape(span * rows, 2 * HD),
                    key_pos <= query_pos,
                )

            @pl.when(step > s // span)
            def _():
                block = kv_all[xx, pl.ds(y0, half), :, pl.ds(tok, rows - tok), :]
                update(h, block.reshape(span * (rows - tok), 2 * HD), None)

            return carry

        lax.fori_loop(0, 2 * NX, visit, 0)
        result = accum[h, :, :HD] / accum[h, :, HD:]
        for g in range(group):
            attended[h, :, g * HD : (g + 1) * HD] = result[g * few : (g + 1) * few].astype(
                jnp.bfloat16
            )

    for at, order in enumerate(KEYING[1:]):
        visit_cache(2 * at, 2 * at + 2)
        go(order)
    drain(kv_run)

    odd = z % 2

    def to(k):
        return {"head": (z + k + NZ) % NZ}

    def columns(h, k):
        zz = (z + k + NZ) % NZ
        block = w_out_all[zz // 2, pl.ds(half * (zz % 2), half)].reshape(width, -1)
        return lax.dot_general(
            attended[h], block, (((1,), (1,)), ((), ())), preferred_element_type=jnp.float32
        )

    def share(h, at, value, there, k):
        parts[h, at] = value.astype(jnp.bfloat16)
        return sends.start(parts.at[h, at], there, to(k))

    def share_out(h):
        relays = [
            share(h, 0, columns(h, 4), relayed.at[h, 2], 2 - 4 * odd),
            share(h, 1, columns(h, 3), relayed.at[h, 0], 1),
            share(h, 2, columns(h, -3), relayed.at[h, 1], -1),
        ]
        ends = [
            share(h, 3, columns(h, 1), arrived.at[h, 2], 1),
            share(h, 4, columns(h, -1), arrived.at[h, 3], -1),
        ]
        for at, k in enumerate((2, -2, 0)):
            sums[h, at] = columns(h, k)
        return relays, ends

    def pass_on(h, relays, ends):
        wait_all(relays)
        sums[h, odd] += relayed[h, 2].astype(jnp.float32)
        for at, k in enumerate((2, -2)):
            value = sums[h, at] + relayed[h, at].astype(jnp.float32)
            ends.append(share(h, 5 + at, value, arrived.at[h, at], k))

    def finish(h, ends):
        wait_all(ends)
        mixed = sums[h, 2]
        for at in range(4):
            mixed = mixed + arrived[h, at].astype(jnp.float32)
        out[h * few : (h + 1) * few, :] = mixed.astype(jnp.bfloat16)

    visit_new(0)
    drain(out_run)
    relays, ends = share_out(0)
    visit_new(1)
    pass_on(0, relays, ends)
    relays_last, ends_last = share_out(1)
    finish(0, ends)
    pass_on(1, relays_last, ends_last)
    finish(1, ends_last)
    sends.finish()


def on_device(
    text_rows,
    picture_rows,
    picture_slots,
    norm_gain,
    w_query,
    w_key,
    w_value,
    w_out,
    cache_keys,
    cache_values,
    recompute_rows,
    recompute_slots,
):
    tok, width = text_rows.shape
    rec_count = recompute_rows.shape[0]
    cache_rows = cache_keys.shape[0]
    group = w_query.shape[1] // HD
    rows = tok + 16
    freqs = ROPE_BASE ** (-(np.arange(HD) % (HD // 2)) / (HD // 2))
    plane = (NX, NY, NC)
    bf16, f32 = jnp.bfloat16, jnp.float32
    few = tok // 2
    in_cols = w_query.shape[1] + w_key.shape[1] + w_value.shape[1]
    copies = PIC_COPIES + 4 * PLANE_COPIES + 2 * LINE_COPIES + 14
    vmem = pl.BlockSpec(memory_space=pltpu.VMEM)
    anywhere = pl.BlockSpec(memory_space=pl.ANY)
    given = (
        picture_rows,
        text_rows,
        recompute_rows,
        w_query,
        w_key,
        w_value,
        w_out.T,
        cache_keys,
        cache_values,
    )
    small = (
        norm_gain[None, :],
        jnp.asarray(freqs[None, :], jnp.float32),
        picture_slots[None, :],
        recompute_slots[None, :],
    )
    return pl.pallas_call(
        functools.partial(block_kernel, (tok, width, rec_count, cache_rows, group)),
        out_shape=jax.ShapeDtypeStruct((tok, width), bf16),
        in_specs=[anywhere] * len(given) + [vmem] * len(small),
        out_specs=vmem,
        scratch_shapes=[
            pltpu.VMEM((picture_rows.shape[0], width + HD), bf16),
            pltpu.VMEM((tok, width), bf16),
            pltpu.VMEM((rec_count, width), bf16),
            pltpu.VMEM((w_query.shape[0], in_cols), bf16),
            pltpu.VMEM(w_out.shape[::-1], bf16),
            pltpu.VMEM((cache_rows, 2 * HD), bf16),
            pltpu.VMEM((rows, 2 * HD), f32),
            pltpu.VMEM((cache_rows, 2 * HD), bf16),
            pltpu.VMEM((2, rows, width // 2), bf16),
            pltpu.VMEM((rows, 2 * HD), bf16),
            pltpu.VMEM(plane + (picture_rows.shape[0], width + HD), bf16),
            pltpu.VMEM((2, NZ, rows, width // 2), bf16),
            pltpu.VMEM(plane + (w_query.shape[0], in_cols), bf16),
            pltpu.VMEM(plane + w_out.shape[::-1], bf16),
            pltpu.VMEM(plane + (cache_rows, 2 * HD), bf16),
            pltpu.VMEM(plane + (rows, 2 * HD), bf16),
            pltpu.VMEM((rows, 1), f32),
            pltpu.VMEM((2, group * few, HD), bf16),
            pltpu.VMEM((2, group * few, 1), f32),
            pltpu.VMEM((2, group * few, 2 * HD), f32),
            pltpu.VMEM((2, few, group * HD), bf16),
            pltpu.VMEM((2, 7, few, width), bf16),
            pltpu.VMEM((2, 3, few, width), f32),
            pltpu.VMEM((2, 3, few, width), bf16),
            pltpu.VMEM((2, 4, few, width), bf16),
            pltpu.SemaphoreType.DMA((copies,)),
            pltpu.SemaphoreType.DMA((copies,)),
            pltpu.SemaphoreType.DMA((7,)),
            pltpu.SemaphoreType.DMA((len(given),)),
        ],
        compiler_params=pltpu.CompilerParams(
            collective_id=0, has_side_effects=True, vmem_limit_bytes=56 * 1024 * 1024
        ),
    )(*given, *small)


def solution(mesh):
    return jax.shard_map(
        on_device,
        mesh=mesh,
        in_specs=(
            P("seq", "head"),
            P("seq", "head"),
            P("seq"),
            P(),
            P("seq", "head"),
            P("seq", "head"),
            P("seq", "head"),
            P("head", "seq"),
            P("seq", "head"),
            P("seq", "head"),
            P("seq", "head"),
            P("seq"),
        ),
        out_specs=P("seq", "head"),
        check_vma=False,
    )
```

time: 145 us -> 136 us (0.938)
  other arithmetic: 3.72 us -> 0 us
  local copies, waits for them, and re-layouts: 3.95 us -> 1.57 us
  Pallas kernels: 136 us -> 134 us
    concatenate x4 -> x0, other arithmetic: 2.65 us -> none  [the longest x1 0.77 us: on_device(): jnp.concatenate([cosine, cosine], axis=1)]
    pallas_call x1, Pallas kernels: 136 us -> 134 us  [on_device(): pl.pallas_call(functools.partial(block_kernel, (tok, width, rec_count, ca...]
    unnamed x19 -> x1, local copies, waits for them, and re-layouts: 3.17 us -> 1.57 us
where the time goes in v3:
time: 136 us
  Pallas kernels  134 us (99%)
  local copies, waits for them, and re-layouts  1.57 us (1%)
    pallas_call x1, Pallas kernels, on_device(): pl.pallas_call(functools.partial(block_kernel, (tok, width, rec_count, ca...  134 us

profile of v3, /device:TPU:7, one launch (start us, length us, event | category | flops | bytes accessed | tf_op | source)
XLA Modules:
  0.0 135.6 jit_solution(8592530522405200142)
XLA Ops:
  0.0 134.0 %shard_map.127 = bf16[128,512]{1,0:T(8,128)(2,1)} custom-call(bf16[32,512]{1,0:T(8,128)(2,1)} %refs_0_.1, bf16[128,512]{1,0:T(8,128)(2,1)} %refs_1_.1, bf16[8,512]{1,0:T(8,128)(2,1)} %refs_2_.1, bf16[64,512]{1,0:T(8,128)(2,1)} %refs_3_.1, bf16[64,128]{1,0:T(8,128)(2,1)} %refs_4_.1, bf16[64,128]{1,0:T(8,128)(2,1)} %refs_5_.1, bf16[64,512]{1,0:T(8,128)(2,1)} %bitcast.4, ...), custom_call_target="tpu_custom_call" | custom-call | tf_op jit(solution)/shard_map/pallas_call | solution.py:566
  134.0 1.6 %copy.15 = bf16[128,512]{1,0:T(8,128)(2,1)} copy(bf16[128,512]{1,0:T(8,128)(2,1)} %shard_map.127) | data formatting | bytes 262144

commit v4 on v3

--- a/solution.py
+++ b/solution.py
@@ -31,7 +31,8 @@
 
 class Sends:
     def __init__(self, send_sems, recv_sems):
-        self.send_sems, self.recv_sems, self.made = send_sems, recv_sems, []
+        self.send_sems, self.recv_sems = send_sems, recv_sems
+        self.made, self.settled = [], 0
 
     def start(self, src, dst, device_id):
         at = len(self.made)
@@ -47,9 +48,11 @@
         self.made.append(copy)
         return copy
 
-    def finish(self):
-        for copy in self.made:
+    def settle(self, count=None):
+        count = len(self.made) if count is None else count
+        for copy in self.made[self.settled : count]:
             copy.wait_send()
+        self.settled = count
 
 
 def wait_all(copies):
@@ -93,6 +96,9 @@
 
     def b_block(k, xx=x):
         return out.at[xx, col(k), c, b_rows]
+
+    def column(k):
+        return out.at[every_x, col(k), c]
 
     def spread(k, source=None):
         source = b_block(k) if source is None else source
@@ -125,8 +131,6 @@
     wait_all(ring_b)
     ring_b = ring_far(y, b_block, up, sends)
     near_spread = [spread(k) for k in NEAR]
-    if split:
-        hand(a_block(0))
     wait_all(own_spread)
     own_forward = forward(0)
     yield
@@ -139,11 +143,8 @@
     for k, copies in zip(NEAR, near_spread):
         wait_all(copies)
         near_forward.append(forward(k))
-    if split:
-        for k in NEAR:
-            hand(a_block(k))
     wait_all([own_forward])
-    hand(b_block(0, every_x))
+    hand(column(0))
     yield
     far_forward = []
     for k, copies in zip(FAR, far_spread):
@@ -151,15 +152,13 @@
         far_forward.append(forward(k))
     if split:
         wait_all(ring_a)
-        for k in FAR:
-            hand(a_block(k))
     for k, copy in zip(NEAR, near_forward):
         wait_all([copy])
-        hand(b_block(k, every_x))
+        hand(column(k))
     yield
     for k, copy in zip(FAR, far_forward):
         wait_all([copy])
-        hand(b_block(k, every_x))
+        hand(column(k))
     yield
     wait_all(handed)
 
@@ -214,8 +213,11 @@
 NORMING = "co"
 KEYING = ("c", "ko", "ko", "ko", "kko")
 
+OUT_SPLIT = 16
+KEY_SPLIT = 32
+
 PIC_COPIES = 39
-PLANE_COPIES = 57
+PLANE_COPIES = 49
 LINE_COPIES = 7
 
 
@@ -280,7 +282,7 @@
     sends = Sends(send_sems, recv_sems)
     pic_run = plane_steps(pics, pics_all, sends, local_sems.at[0], 0)
     in_run = plane_steps(w_in, w_in_all, sends, local_sems.at[1], 16)
-    out_run = plane_steps(w_out, w_out_all, sends, local_sems.at[2], 16)
+    out_run = plane_steps(w_out, w_out_all, sends, local_sems.at[2], OUT_SPLIT)
     cache_run = plane_steps(cache_own, cache_all, sends, local_sems.at[3], 16)
     runs = {"p": pic_run, "i": in_run, "o": out_run, "c": cache_run}
 
@@ -378,7 +380,8 @@
     valid = lax.broadcasted_iota(jnp.int32, (rows - tok, 1), 0) < rec_count
     kv_own[tok:, :HD] = jnp.where(valid, fresh[:, :HD], fresh[:1, :HD]).astype(jnp.bfloat16)
     kv_own[tok:, HD:] = jnp.where(valid, fresh[:, HD:], ABSENT).astype(jnp.bfloat16)
-    kv_run = plane_steps(kv_own, kv_all, sends, local_sems.at[6], 32)
+    early = len(sends.made)
+    kv_run = plane_steps(kv_own, kv_all, sends, local_sems.at[6], KEY_SPLIT)
     advance(kv_run)
     runs["k"] = kv_run
     go(KEYING[0])
@@ -395,12 +398,12 @@
     span = half * NC
 
     def update(h, block, mask):
-        keys = block[:, :HD]
-        values = block[:, HD:].astype(jnp.float32)
-        present = values < ABSENT / 2
+        keys, values = block[:, :HD], block[:, HD:]
+        present = values < jnp.bfloat16(ABSENT / 2)
+        zero = jnp.zeros_like(values)
         values = jnp.concatenate(
-            [jnp.where(present, values, 0.0), jnp.where(present, 1.0, 0.0)], axis=1
-        ).astype(jnp.bfloat16)
+            [jnp.where(present, values, zero), jnp.where(present, zero + 1, zero)], axis=1
+        )
         scores = lax.dot_general(
             queries[h], keys, (((1,), (1,)), ((), ())), preferred_element_type=jnp.float32
         )
@@ -460,6 +463,8 @@
 
     for at, order in enumerate(KEYING[1:]):
         visit_cache(2 * at, 2 * at + 2)
+        if at < 3:
+            sends.settle(early * (at + 1) // 3)
         go(order)
     drain(kv_run)
 
@@ -509,14 +514,16 @@
 
     visit_new(0)
     drain(out_run)
+    before = len(sends.made)
     relays, ends = share_out(0)
     visit_new(1)
     pass_on(0, relays, ends)
     relays_last, ends_last = share_out(1)
+    sends.settle(before)
     finish(0, ends)
     pass_on(1, relays_last, ends_last)
     finish(1, ends_last)
-    sends.finish()
+    sends.settle()
 
 
 def on_device(

time: 136 us -> 135 us (level)
  no operation moved by 1% of the time
where the time goes in v4:
time: 135 us
  Pallas kernels  133 us (99%)
  local copies, waits for them, and re-layouts  1.57 us (1%)
    pallas_call x1, Pallas kernels, on_device(): pl.pallas_call(functools.partial(block_kernel, (tok, width, rec_count, ca...  133 us

profile of v4, /device:TPU:7, one launch (start us, length us, event | category | flops | bytes accessed | tf_op | source)
XLA Modules:
  0.0 134.8 jit_solution(4229295194442575209)
XLA Ops:
  0.0 133.2 %shard_map.127 = bf16[128,512]{1,0:T(8,128)(2,1)} custom-call(bf16[32,512]{1,0:T(8,128)(2,1)} %refs_0_.1, bf16[128,512]{1,0:T(8,128)(2,1)} %refs_1_.1, bf16[8,512]{1,0:T(8,128)(2,1)} %refs_2_.1, bf16[64,512]{1,0:T(8,128)(2,1)} %refs_3_.1, bf16[64,128]{1,0:T(8,128)(2,1)} %refs_4_.1, bf16[64,128]{1,0:T(8,128)(2,1)} %refs_5_.1, bf16[64,512]{1,0:T(8,128)(2,1)} %bitcast.4, ...), custom_call_target="tpu_custom_call" | custom-call | tf_op jit(solution)/shard_map/pallas_call | solution.py:573
  133.2 1.6 %copy.15 = bf16[128,512]{1,0:T(8,128)(2,1)} copy(bf16[128,512]{1,0:T(8,128)(2,1)} %shard_map.127) | data formatting | bytes 262144

commit v5 on v4

--- a/solution.py
+++ b/solution.py
@@ -426,7 +426,7 @@
 
         lax.fori_loop(first, last, visit, 0)
 
-    def visit_new(h):
+    def visit_new(h, first, last):
         def visit(step, carry):
             xx, y0 = step // 2, half * (step % 2)
 
@@ -454,7 +454,9 @@
 
             return carry
 
-        lax.fori_loop(0, 2 * NX, visit, 0)
+        lax.fori_loop(first, last, visit, 0)
+
+    def close(h):
         result = accum[h, :, :HD] / accum[h, :, HD:]
         for g in range(group):
             attended[h, :, g * HD : (g + 1) * HD] = result[g * few : (g + 1) * few].astype(
@@ -512,12 +514,15 @@
             mixed = mixed + arrived[h, at].astype(jnp.float32)
         out[h * few : (h + 1) * few, :] = mixed.astype(jnp.bfloat16)
 
-    visit_new(0)
+    visit_new(0, 0, 2 * NX)
+    close(0)
     drain(out_run)
     before = len(sends.made)
     relays, ends = share_out(0)
-    visit_new(1)
+    visit_new(1, 0, 2 * NX - 2)
     pass_on(0, relays, ends)
+    visit_new(1, 2 * NX - 2, 2 * NX)
+    close(1)
     relays_last, ends_last = share_out(1)
     sends.settle(before)
     finish(0, ends)

time: 135 us -> 133 us (0.985)
    pallas_call x1, Pallas kernels: 133 us -> 132 us  [on_device(): pl.pallas_call(functools.partial(block_kernel, (tok, width, rec_count, ca...]
where the time goes in v5:
time: 133 us
  Pallas kernels  132 us (99%)
  local copies, waits for them, and re-layouts  1.57 us (1%)
    pallas_call x1, Pallas kernels, on_device(): pl.pallas_call(functools.partial(block_kernel, (tok, width, rec_count, ca...  132 us

profile of v5, /device:TPU:7, one launch (start us, length us, event | category | flops | bytes accessed | tf_op | source)
XLA Modules:
  0.0 133.3 jit_solution(3423475534932023764)
XLA Ops:
  0.0 131.7 %shard_map.127 = bf16[128,512]{1,0:T(8,128)(2,1)} custom-call(bf16[32,512]{1,0:T(8,128)(2,1)} %refs_0_.1, bf16[128,512]{1,0:T(8,128)(2,1)} %refs_1_.1, bf16[8,512]{1,0:T(8,128)(2,1)} %refs_2_.1, bf16[64,512]{1,0:T(8,128)(2,1)} %refs_3_.1, bf16[64,128]{1,0:T(8,128)(2,1)} %refs_4_.1, bf16[64,128]{1,0:T(8,128)(2,1)} %refs_5_.1, bf16[64,512]{1,0:T(8,128)(2,1)} %bitcast.4, ...), custom_call_target="tpu_custom_call" | custom-call | tf_op jit(solution)/shard_map/pallas_call | solution.py:578
  131.7 1.6 %copy.15 = bf16[128,512]{1,0:T(8,128)(2,1)} copy(bf16[128,512]{1,0:T(8,128)(2,1)} %shard_map.127) | data formatting | bytes 262144
